TPU v7x, 256 devices: a whole 4x4x8 slice. The times are simulated.
256 devices in a mesh: gx: 16 (over y, x_hi, core), gy: 16 (over z, x_lo).
Axes of the slice: x: 4 (x_hi: 2, x_lo: 2; x = x_hi * 2 + x_lo), y: 4, z: 8, core: 2. Of those that a mesh axis runs over, the one named last changes fastest.
Arguments:
- inputs: bfloat16 [256, 16, 48, 512], P(('gx', 'gy')), may hold values from -6 to 6
- grad_out: bfloat16 [256, 16, 48, 512], P(('gx', 'gy')), may hold values from -6 to 6
- conv_kernel: float32 [7, 7, 512], replicated, may hold values from -0.875 to 0.875
- conv_bias: float32 [512], replicated, may hold values from -4 to 4
- layer_norm_gain: float32 [512], replicated, may hold values from 0.1 to 1.9
- layer_norm_bias: float32 [512], replicated, may hold values from -3 to 3
- w_up: bfloat16 [512, 2048], replicated, may hold values from -0.25 to 0.25
- up_bias: float32 [2048], replicated, may hold values from -3 to 3
- w_down: bfloat16 [512, 2048], replicated, may hold values from -0.125 to 0.125
- down_bias: float32 [512], replicated, may hold values from -3 to 3
- layer_scale: float32 [512], replicated, may hold values from 0.1 to 1
Outputs:
- grad_inputs: bfloat16 [256, 16, 48, 512], P(('gx', 'gy'))
- grad_kernel: float32 [7, 7, 512], replicated
- grad_conv_bias: float32 [512], replicated
- grad_ln_gain: float32 [512], replicated
- grad_ln_bias: float32 [512], replicated
- grad_w_up: float32 [512, 2048], replicated
- grad_up_bias: float32 [2048], replicated
- grad_w_down: float32 [512, 2048], replicated
- grad_down_bias: float32 [512], replicated
- grad_layer_scale: float32 [512], replicated
All inputs are finite; a program needn't handle non-finite values.
Results may differ from a plain program's by a relative error of at most 0.0063.
Values sent between devices are 32-bit elements; how exact they have to be, the bound alone decides.
No kernel may reach another device: no remote copies, remote signals or barrier semaphores. Data moves between devices by JAX's collectives and lax.ppermute only.
A program may use at most 128 MiB of HBM per device.

v0:
```python
import jax
import jax.numpy as jnp
from jax import lax
from jax.experimental import pallas as pl
from jax.experimental.pallas import tpu as pltpu
from jax.sharding import Mesh
from jax.sharding import PartitionSpec as P


AXES = ("y", "xh", "c", "z", "xl")
XAX = ("xh", "xl")
PLANE = ("y", "xh", "xl")
RING4 = [[(i, (i + s) % 4) for i in range(4)] for s in range(4)]
FLIP = [(0, 1), (1, 0)]


def gelu_cdf(pre):
    return 0.5 * (1.0 + lax.erf(pre * 0.7071067811865476))


def gelu_slope(pre):
    cdf = gelu_cdf(pre)
    dens = jnp.exp(-0.5 * pre * pre) * 0.3989422804014327
    return cdf + pre * dens


def coords():
    x = lax.axis_index("xh") * 2 + lax.axis_index("xl")
    return lax.axis_index("c"), x, lax.axis_index("y")


def after(value, *others):
    return lax.optimization_barrier((value,) + others)[0]


def own_half_last(channels):
    c = lax.axis_index("c")
    low, high = channels[:, :256], channels[:, 256:]
    return jnp.where(c == 0, high, low), jnp.where(c == 0, low, high)


def contract(left, right):
    return lax.dot_general(
        left, right, (((0,), (0,)), ((), ())), preferred_element_type=jnp.float32
    )


def scatter_z(piece):
    width = piece.shape[1]
    moved = lax.all_to_all(piece.reshape(8, 2, width), "z", 0, 0, tiled=True)
    return jnp.sum(moved, axis=0, keepdims=True)


def gather_z(summed):
    width = summed.shape[2]
    full = lax.all_to_all(jnp.broadcast_to(summed, (8, 2, width)), "z", 0, 0, tiled=True)
    return full.reshape(16, width)


def double_z(piece):
    for step in (1, 2, 4):
        piece = piece + lax.ppermute(piece, "z", [(i, i ^ step) for i in range(8)])
    return piece


def gather_near(piece):
    return [
        jnp.concatenate([p] + [lax.ppermute(p, ax, RING4[s]) for s in (1, 2, 3)], axis=0)
        for p, ax in ((piece[:8], "y"), (piece[8:], XAX))
    ]


def gather_sides(near):
    return [
        (lax.ppermute(p, ax, RING4[1]), lax.ppermute(p, ax, RING4[3]))
        for p, ax in zip(near, (XAX, "y"))
    ]


def gather_rest(near, sides):
    out = []
    for p, (below, above), ax in zip(near, sides, (XAX, "y")):
        far = (lax.ppermute(below[:16], ax, RING4[1]), lax.ppermute(above[16:], ax, RING4[3]))
        out += [p, below, above, far[0], far[1]]
    return out, [lax.ppermute(p, "c", FLIP) for p in out]


def place_kernel(far, where, *refs):
    pieces, outs, sem = refs[:10], refs[-4:-1], refs[-1]
    core, x, y = where[0], where[1], where[2]
    half = core if far == 0 else 1 - core
    copies = []

    def copy(src, dst):
        copies.append(pltpu.make_async_copy(src, dst, sem.at[len(copies)]))

    for part in range(2):
        first, second = (x, y) if part == 0 else (y, x)
        for k, (s1, low, count) in enumerate(
            ((0, 0, 4), (1, 0, 4), (3, 0, 4), (2, 0, 2), (2, 2, 2))
        ):
            p1 = lax.rem(first + 4 - s1, 4)
            for s2 in range(low, low + count):
                p2 = lax.rem(second + 4 - s2, 4)
                at = p2 * 4 + p1 if part == 0 else p1 * 4 + p2
                src = pieces[part * 5 + k].at[pl.ds((s2 - low) * 8, 8), :]
                row = pl.multiple_of(half * 256 + at * 16 + part * 8, 8)
                copy(src.at[:, pl.ds(0, 2048)], outs[0].at[pl.ds(row, 8), :])
                copy(src.at[:, pl.ds(2048, 2048)], outs[1].at[pl.ds(row, 8), :])
                if part == 0:
                    row = pl.multiple_of(half * 32 + p1 * 8, 8)
                    lane = pl.multiple_of(p2 * 128, 128)
                    copy(
                        src.at[:, pl.ds(4096, 128)],
                        outs[2].at[pl.ds(row, 8), pl.ds(lane, 128)],
                    )
    for c in copies:
        c.start()
    for c in copies:
        c.wait()


def place(own, other):
    c, x, y = coords()
    where = jnp.stack([c, x, y]).astype(jnp.int32)
    vmem = pl.BlockSpec(memory_space=pltpu.VMEM)
    anywhere = pl.BlockSpec(memory_space=pl.ANY)
    shapes = tuple(
        jax.ShapeDtypeStruct(sh, jnp.float32) for sh in ((512, 2048), (512, 2048), (64, 512))
    )

    def call(far, pieces, whole):
        return pl.pallas_call(
            lambda *refs: place_kernel(far, *refs),
            out_shape=shapes,
            in_specs=[pl.BlockSpec(memory_space=pltpu.SMEM)] + [vmem] * 10 + [anywhere] * len(whole),
            out_specs=(anywhere,) * 3,
            scratch_shapes=[pltpu.SemaphoreType.DMA((80,))],
            input_output_aliases={11 + i: i for i in range(len(whole))},
        )(where, *pieces, *whole)

    return call(1, other, call(0, own, ()))


def forward_kernel(image, kernel, bias, gain, shift, xhat, normed, inv, pad):
    pad[...] = jnp.zeros_like(pad)

    @pl.loop(0, 16)
    def _(h):
        for b in range(4):
            pad[b, h + 3, pl.ds(8, 48), :] = image[h, :, b * 128 : b * 128 + 128].astype(
                jnp.float32
            )

    for b in range(4):
        lanes = slice(b * 128, b * 128 + 128)

        @pl.loop(0, 4)
        def _(group):
            h = group * 4
            acc = [jnp.broadcast_to(bias[:, lanes], (48, 128))] * 4
            for r in range(10):
                for j in range(7):
                    v = pad[b, h + r, pl.ds(5 + j, 48), :]
                    for k in range(4):
                        if 0 <= r - k < 7:
                            acc[k] = acc[k] + v * kernel[r - k, j : j + 1, lanes]
            for k in range(4):
                xhat[pl.ds(pl.multiple_of((h + k) * 48, 48), 48), lanes] = acc[k]

    @pl.loop(0, 16)
    def _(h):
        rows = pl.ds(pl.multiple_of(h * 48, 48), 48)
        mixed = xhat[rows, :]
        mixed = mixed - jnp.mean(mixed, axis=-1, keepdims=True)
        rest = lax.rsqrt(jnp.mean(mixed * mixed, axis=-1, keepdims=True) + 1e-06)
        inv[rows, :] = rest
        unit = mixed * rest
        xhat[rows, :] = unit
        normed[rows, :] = (unit * gain[...] + shift[...]).astype(jnp.bfloat16)


def forward(image, kernel, bias, gain, shift):
    return pl.pallas_call(
        forward_kernel,
        out_shape=(
            jax.ShapeDtypeStruct((768, 512), jnp.float32),
            jax.ShapeDtypeStruct((768, 512), jnp.bfloat16),
            jax.ShapeDtypeStruct((768, 1), jnp.float32),
        ),
        scratch_shapes=[pltpu.VMEM((4, 22, 64, 128), jnp.float32)],
        compiler_params=pltpu.CompilerParams(vmem_limit_bytes=40 << 20),
        name="conv_norm",
    )(image, kernel, bias, gain, shift)


def backward_kernel(gn, xhat, inv, gain, image, upstream, kernel, out, taps, pad, sums, acc):
    pad[...] = jnp.zeros_like(pad)
    sums[...] = jnp.zeros_like(sums)

    def fold(v):
        return jnp.sum(v.reshape(6, 8, 128), axis=0)

    @pl.loop(0, 16)
    def _(h):
        rows = pl.ds(pl.multiple_of(h * 48, 48), 48)
        rest = inv[rows, :]
        gx, xs = [], []
        for b in range(4):
            lanes = slice(b * 128, b * 128 + 128)
            g, x = gn[rows, lanes], xhat[rows, lanes]
            sums[0, :, lanes] += fold(g * x)
            sums[1, :, lanes] += fold(g)
            gx.append(g * gain[:, lanes])
            xs.append(x)
        plain = gx[0] + gx[1] + gx[2] + gx[3]
        cross = gx[0] * xs[0] + gx[1] * xs[1] + gx[2] * xs[2] + gx[3] * xs[3]
        m1 = jnp.sum(plain, axis=-1, keepdims=True) * (1.0 / 512)
        m2 = jnp.sum(cross, axis=-1, keepdims=True) * (1.0 / 512)
        for b in range(4):
            gm = rest * (gx[b] - m1 - xs[b] * m2)
            sums[2, :, b * 128 : b * 128 + 128] += fold(gm)
            pad[b, h + 3, pl.ds(8, 48), :] = gm

    for b in range(4):
        lanes = slice(b * 128, b * 128 + 128)
        acc[...] = jnp.zeros_like(acc)

        @pl.loop(0, 16)
        def _(h):
            x = image[h, :, lanes].astype(jnp.float32)
            back = upstream[h, :, lanes].astype(jnp.float32)
            for i in range(7):
                for j in range(7):
                    t = i * 7 + j
                    g = pad[b, h + 6 - i, pl.ds(11 - j, 48), :]
                    back = back + g * kernel[i, j : j + 1, lanes]
                    acc[t] += fold(g * x)
            out[h, :, lanes] = back.astype(jnp.bfloat16)

        for t in range(49):
            taps[t : t + 1, lanes] = jnp.sum(acc[t], axis=0, keepdims=True) * (1.0 / 256)

    for t in range(3):
        taps[49 + t : 50 + t, :] = jnp.sum(sums[t], axis=0, keepdims=True) * (1.0 / 256)


def backward(gn, xhat, inv, gain, image, upstream, kernel):
    return pl.pallas_call(
        backward_kernel,
        out_shape=(
            jax.ShapeDtypeStruct((16, 48, 512), jnp.bfloat16),
            jax.ShapeDtypeStruct((52, 512), jnp.float32),
        ),
        scratch_shapes=[
            pltpu.VMEM((4, 22, 64, 128), jnp.float32),
            pltpu.VMEM((3, 8, 512), jnp.float32),
            pltpu.VMEM((49, 8, 128), jnp.float32),
        ],
        compiler_params=pltpu.CompilerParams(vmem_limit_bytes=40 << 20),
        cost_estimate=pl.CostEstimate(flops=80000000, bytes_accessed=6000000, transcendentals=0),
        name="conv_back",
    )(gn, xhat, inv, gain, image, upstream, kernel)


def body(
    inputs,
    grad_out,
    conv_kernel,
    conv_bias,
    layer_norm_gain,
    layer_norm_bias,
    w_up,
    up_bias,
    w_down,
    down_bias,
    layer_scale,
):
    image = inputs[0]
    row_count, column_count, channel_count = image.shape
    ksize = conv_kernel.shape[0]
    scale = 1.0 / 256
    gain_row = layer_norm_gain.reshape(1, 512)
    standardized_input, normalized_output, inverse_deviation = forward(
        image, conv_kernel, conv_bias.reshape(1, 512), gain_row, layer_norm_bias.reshape(1, 512)
    )
    pre = jnp.dot(normalized_output, w_up, preferred_element_type=jnp.float32) + up_bias
    hidden = (pre * gelu_cdf(pre)).astype(jnp.bfloat16)
    upstream = grad_out[0].astype(jnp.float32).reshape(row_count * column_count, channel_count)
    g_branch = (upstream * layer_scale).astype(jnp.bfloat16)

    gb_send, gb_keep = own_half_last(g_branch)
    down_send = contract(gb_send, hidden) * scale
    down_keep = contract(gb_keep, hidden) * scale
    down_mine = down_keep + lax.ppermute(down_send, "c", FLIP)

    g_branch_b, pre, _ = lax.optimization_barrier((g_branch, pre, down_send))
    g_hidden = jnp.dot(g_branch_b, w_down, preferred_element_type=jnp.float32)
    g_pre = (g_hidden * gelu_slope(pre)).astype(jnp.bfloat16)

    g_pre, down_mine = lax.optimization_barrier((g_pre, down_mine))
    moved = lax.all_to_all(down_mine.reshape(16, 16, 2048), PLANE, 0, 0, tiled=True)
    norm_send, norm_keep = own_half_last(normalized_output)
    up_send = contract(norm_send, g_pre) * scale
    up_keep = contract(norm_keep, g_pre) * scale
    up_recv = lax.ppermute(up_send, "c", FLIP)

    g_pre_b = after(g_pre, up_keep)
    normalized_gradient = lax.dot_general(
        g_pre_b, w_up, (((1,), (1,)), ((), ())), preferred_element_type=jnp.float32
    )
    grad_inputs, block = backward(
        normalized_gradient,
        standardized_input,
        inverse_deviation,
        gain_row,
        image,
        grad_out[0],
        conv_kernel,
    )
    grad_inputs = grad_inputs.reshape(1, row_count, column_count, channel_count)

    hidden_b, g_pre_c, upstream, _ = lax.optimization_barrier((hidden, g_pre, upstream, up_keep))
    g_up_bias = jnp.sum(g_pre_c.astype(jnp.float32), axis=0)
    branch = (
        lax.dot_general(
            hidden_b, w_down, (((1,), (1,)), ((), ())), preferred_element_type=jnp.float32
        )
        + down_bias
    )
    g_scale = jnp.sum(upstream * branch, axis=0)
    g_down_bias = jnp.sum((upstream * layer_scale).astype(jnp.bfloat16).astype(jnp.float32), axis=0)
    rows = jnp.concatenate([g_down_bias, g_scale, g_up_bias]).reshape(6, 512) * scale
    block = jnp.concatenate([block, rows, jnp.zeros((6, 512), jnp.float32)], axis=0)
    c = lax.axis_index("c")
    small_send = jnp.where(c == 0, block[32:], block[:32])
    small_keep = jnp.where(c == 0, block[:32], block[32:])
    small_mine = small_keep + lax.ppermute(small_send, "c", FLIP)
    small_mine = small_mine.reshape(4, 8, 4, 128).transpose(2, 0, 1, 3).reshape(16, 8, 128)
    small_mine = jnp.pad(small_mine, ((0, 0), (0, 8), (0, 0)))
    up_mine = jnp.concatenate([(up_keep + up_recv).reshape(16, 16, 2048), small_mine], axis=2)

    up_mine, moved, grad_inputs = lax.optimization_barrier((up_mine, moved, grad_inputs))
    down_piece = jnp.sum(moved, axis=0)
    up_piece = jnp.sum(lax.all_to_all(up_mine, PLANE, 0, 0, tiled=True), axis=0)
    down_full = double_z(down_piece)

    up_piece, down_full = lax.optimization_barrier((up_piece, down_full))
    up_full = gather_z(scatter_z(up_piece))
    near = gather_near(jnp.concatenate([down_full, up_full], axis=1))
    own, other = gather_rest(near, gather_sides(near))
    gw_down, gw_up, block = place(own, other)
    return (
        grad_inputs,
        block[:49].reshape(ksize, ksize, channel_count),
        block[51],
        block[49],
        block[50],
        gw_up,
        block[54:58].reshape(-1),
        gw_down,
        block[52],
        block[53],
    )


def solution(mesh):
    fine = Mesh(mesh.devices.reshape(4, 2, 2, 8, 2), AXES)
    image = P(AXES, None, None, None)
    return jax.shard_map(
        body,
        mesh=fine,
        in_specs=(image, image) + (P(),) * 9,
        out_specs=(image,) + (P(),) * 9,
        check_vma=False,
    )
```

profile of v0, /device:TPU:1, one launch (start us, length us, event | category | flops | bytes accessed | tf_op | source)
XLA Modules:
  0.0 204.0 jit_solution(9353802123688492250)
XLA Ops:
  0.7 1.4 multiply_convert_fusion.2
  2.1 1.1 copy-done.2
  6.2 8.6 %conv_norm.1 = (f32[768,512]{1,0:T(8,128)S(1)}, bf16[768,512]{1,0:T(8,128)(2,1)S(1)}, f32[768,1]{1,0:T(8,128)S(1)}) custom-call(bf16[16,48,512]{2,1,0:T(8,128)(2,1)S(1)} %bitcast.42, f32[7,7,512]{2,1,0:T(8,128)S(1)} %copy-done.6, f32[1,512]{1,0:T(1,128)S(1)} %bitcast.46, f32[1,512]{1,0:T(1,128)S(1)} %bitcast.44, f32[1,512]{1,0:T(1,128)S(1)} %bitcast.47), custom_call_target="tpu_custom_call" | custom-call | tf_op jit(solution)/shard_map/conv_norm/pallas_call | solution.py:184
  14.8 3.2 %multiply_convert_fusion = (bf16[768,2048]{1,0:T(8,128)(2,1)S(1)}, f32[768,2048]{1,0:T(8,128)S(1)}) fusion(f32[2048]{0:T(1024)S(1)} %copy-done.29, bf16[768,512]{1,0:T(8,128)(2,1)S(1)} %get-tuple-element.34, bf16[512,2048]{1,0:T(8,128)(2,1)S(1)} %copy-done), kind=kOutput, calls=%fused_computation.8 | convolution fusion | flops 1620049920 | bytes 12328960 | tf_op jit(solution)/shard_map/dot_general | solution.py:287
  19.1 3.3 %collective-permute-start = (f32[256,2048]{1,0:T(8,128)S(1)}, f32[256,2048]{1,0:T(8,128)S(1)}, u32[]{:S(2)}, u32[]{:S(2)}) collective-permute-start(f32[256,2048]{1,0:T(8,128)S(1)} %convolution_multiply_fusion.2), channel_id=1, source_target_pairs={{0,16},{16,0},{1,17},{17,1},{2,18},{18,2},{3,19},{19,3},{4,20},{20... | collective-permute-start | bytes 6291464 | tf_op jit(solution)/shard_map/ppermute | solution.py:295
  22.4 1.4 bitcast_convert_fusion
  23.8 3.8 %fusion.5 = bf16[768,2048]{1,0:T(8,128)(2,1)S(1)} fusion(f32[768,2048]{1,0:T(8,128)S(1)} %get-tuple-element.36, bf16[768,512]{1,0:T(8,128)(2,1)S(1)} %multiply_convert_fusion.2, bf16[512,2048]{1,0:T(8,128)(2,1)S(1)} %copy-done.28), kind=kOutput, calls=%fused_computation.6 | convolution fusion | flops 1626341376 | bytes 12320768 | tf_op jit(solution)/shard_map/dot_general | solution.py:298
  27.7 2.4 %fusion.6 = f32[256,2048]{1,0:T(8,128)} fusion(f32[256,2048]{1,0:T(8,128)S(1)} %collective-permute-done, bf16[768,2048]{1,0:T(8,128)(2,1)S(1)} %get-tuple-element.43, pred[]{:T(512)S(6)} %eq.2, bf16[768,512]{1,0:T(8,128)(2,1)S(1)} %multiply_convert_fusion.2), kind=kOutput, calls=%fused_computation.13 | convolution fusion | flops 806551552 | bytes 8126465 | tf_op jit(solution)/shard_map/dot_general | solution.py:43
  30.1 2.4 %convolution_multiply_fusion = f32[256,2048]{1,0:T(8,128)} fusion(bf16[768,2048]{1,0:T(8,128)(2,1)S(1)} %fusion.5, pred[]{:T(512)S(6)} %eq.2, bf16[768,512]{1,0:T(8,128)(2,1)S(1)} %get-tuple-element.34), kind=kOutput, calls=%fused_computation.11 | convolution fusion | flops 806027264 | bytes 6029313 | tf_op jit(solution)/shard_map/dot_general | solution.py:43
  32.4 2.4 %broadcast_multiply_fusion = f32[256,2048]{1,0:T(8,128)} fusion(bf16[768,2048]{1,0:T(8,128)(2,1)S(1)} %fusion.5, pred[]{:T(512)S(6)} %eq.2, bf16[768,512]{1,0:T(8,128)(2,1)S(1)} %get-tuple-element.34), kind=kOutput, calls=%fused_computation.21 | convolution fusion | flops 805502976 | bytes 6029313 | tf_op jit(solution)/shard_map/dot_general | solution.py:43
  34.8 5.2 %all-to-all-start = ((f32[16,16,2048]{2,1,0:T(8,128)}), f32[16,16,2048]{2,1,0:T(8,128)}, u32[]{:S(2)}, u32[]{:S(2)}) async-start(f32[16,16,2048]{2,1,0:T(8,128)} %bitcast.49), calls=%async_computation | async-start | bytes 4194304 | tf_op jit(solution)/shard_map/all_to_all | solution.py:302
  41.2 1.9 convert_reduce_fusion.1
  43.1 2.4 %convert_reduce_fusion = f32[2048]{0:T(1024)S(1)} fusion(bf16[768,2048]{1,0:T(8,128)(2,1)} %copy-done.12), kind=kLoop, calls=%fused_computation.7 | loop fusion | flops 3143680 | bytes 3153920 | tf_op jit(solution)/shard_map/reduce_sum | solution.py:324
  45.5 3.4 %multiply_reduce_fusion = f32[512]{0:T(512)S(1)} fusion(f32[768,512]{1,0:T(8,128)S(1)} %copy-done.14, bf16[768,2048]{1,0:T(8,128)(2,1)S(1)} %copy-done.16, bf16[512,2048]{1,0:T(8,128)(2,1)} %param.19, f32[512]{0:T(512)S(1)} %copy-done.30), kind=kOutput, calls=%fused_computation.17 | convolution fusion | flops 1611791872 | bytes 6819840 | tf_op jit(solution)/shard_map/dot_general | solution.py:326
  49.0 3.9 %fusion.27.gn = f32[768,512]{1,0:T(8,128)S(1)} fusion(bf16[768,2048]{1,0:T(8,128)(2,1)} %copy-done.12, bf16[512,2048]{1,0:T(8,128)(2,1)S(1)} %copy-done), kind=kOutput, calls=%fused_computation.54 | convolution fusion | flops 1610612736 | bytes 6815744 | tf_op jit(solution)/shard_map/dot_general | solution.py:309
  52.9 13.6 %conv_back.1 = (bf16[16,48,512]{2,1,0:T(8,128)(2,1)}, f32[52,512]{1,0:T(8,128)S(1)}) custom-call(f32[768,512]{1,0:T(8,128)S(1)} %fusion.27.gn, f32[768,512]{1,0:T(8,128)S(1)} %copy-done.5, f32[768,1]{1,0:T(8,128)S(1)} %get-tuple-element.40.inv, f32[1,512]{1,0:T(1,128)S(1)} %bitcast.45, bf16[16,48,512]{2,1,0:T(8,128)(2,1)S(1)} %bitcast.43, ...), custom_call_target="tpu_custom_call" | custom-call | flops 80000000 | bytes 6000000 | tf_op jit(solution)/shard_map/conv_back/pallas_call | solution.py:249
  66.7 1.2 collective-permute-done.2
  68.0 1.9 multiply_add_fusion
  69.9 1.5 select_maximum_fusion
  71.7 6.4 %all-to-all-start.1 = ((f32[16,16,2176]{2,1,0:T(8,128)}), f32[16,16,2176]{2,1,0:T(8,128)}, u32[]{:S(2)}, u32[]{:S(2)}) async-start(f32[16,16,2176]{2,1,0:T(8,128)} %select_maximum_fusion), calls=%async_computation.1 | async-start | bytes 4456448 | tf_op jit(solution)/shard_map/all_to_all | solution.py:345
  78.1 1.7 reduce_sum.58
  79.8 1.7 collective-permute-start.3
  81.6 3.5 %collective-permute-done.3 = f32[16,2048]{1,0:T(8,128)S(1)} collective-permute-done((f32[16,2048]{1,0:T(8,128)S(1)}, f32[16,2048]{1,0:T(8,128)S(1)}, u32[]{:S(2)}, u32[]{:S(2)}) %collective-permute-start.3) | collective-permute-done | bytes 131104 | tf_op jit(solution)/shard_map/ppermute | solution.py:62
  85.0 3.0 %collective-permute-start.4 = (f32[16,2048]{1,0:T(8,128)S(1)}, f32[16,2048]{1,0:T(8,128)S(1)}, u32[]{:S(2)}, u32[]{:S(2)}) collective-permute-start(f32[16,2048]{1,0:T(8,128)S(1)} %add.59), channel_id=1, source_target_pairs={{0,4},{2,6},{4,0},{6,2},{8,12},{10,14},{12,8},{14,10},{1,5},{3,7},... | collective-permute-start | bytes 393224 | tf_op jit(solution)/shard_map/ppermute | solution.py:62
  88.1 5.9 %collective-permute-done.4 = f32[16,2048]{1,0:T(8,128)S(1)} collective-permute-done((f32[16,2048]{1,0:T(8,128)S(1)}, f32[16,2048]{1,0:T(8,128)S(1)}, u32[]{:S(2)}, u32[]{:S(2)}) %collective-permute-start.4) | collective-permute-done | bytes 131104 | tf_op jit(solution)/shard_map/ppermute | solution.py:62
  94.0 6.6 %collective-permute-start.5 = (f32[16,2048]{1,0:T(8,128)S(1)}, f32[16,2048]{1,0:T(8,128)S(1)}, u32[]{:S(2)}, u32[]{:S(2)}) collective-permute-start(f32[16,2048]{1,0:T(8,128)S(1)} %add.60), channel_id=1, source_target_pairs={{0,8},{2,10},{4,12},{6,14},{8,0},{10,2},{12,4},{14,6},{1,9},{3,11}... | collective-permute-start | bytes 393224 | tf_op jit(solution)/shard_map/ppermute | solution.py:62
  100.6 3.0 %collective-permute-done.5 = f32[16,2048]{1,0:T(8,128)S(1)} collective-permute-done((f32[16,2048]{1,0:T(8,128)S(1)}, f32[16,2048]{1,0:T(8,128)S(1)}, u32[]{:S(2)}, u32[]{:S(2)}) %collective-permute-start.5) | collective-permute-done | bytes 131104 | tf_op jit(solution)/shard_map/ppermute | solution.py:62
  103.6 9.2 %all-to-all-done.1 = f32[16,16,2176]{2,1,0:T(8,128)} async-done(((f32[16,16,2176]{2,1,0:T(8,128)}), f32[16,16,2176]{2,1,0:T(8,128)}, u32[]{:S(2)}, u32[]{:S(2)}) %all-to-all-start.1) | async-done | bytes 2228256 | tf_op jit(solution)/shard_map/all_to_all | solution.py:345
  112.9 1.7 reduce_sum.57
  114.7 16.0 %all_to_all.20 = f32[8,2,2176]{2,1,0:T(2,128)S(1)} all-to-all(f32[8,2,2176]{2,1,0:T(2,128)S(1)} %reshape.75), channel_id=1, replica_groups=mesh['y'=4,'xh'=2,'c'=2,'z'=8,'xl'=2] {'z'}, dimensions={0} | all-to-all | bytes 278528 | tf_op jit(solution)/shard_map/all_to_all | solution.py:50
  131.5 3.4 %all-to-all-start.3 = ((f32[8,2,2176]{2,1,0:T(2,128)}), f32[8,2,2176]{2,1,0:T(2,128)S(1)}, u32[]{:S(2)}, u32[]{:S(2)}) async-start(f32[8,2,2176]{2,1,0:T(2,128)} %broadcast_in_dim.5), calls=%async_computation.3 | async-start | bytes 278528 | tf_op jit(solution)/shard_map/all_to_all | solution.py:56
  134.9 7.9 %all-to-all-done.3 = f32[8,2,2176]{2,1,0:T(2,128)S(1)} async-done(((f32[8,2,2176]{2,1,0:T(2,128)}), f32[8,2,2176]{2,1,0:T(2,128)S(1)}, u32[]{:S(2)}, u32[]{:S(2)}) %all-to-all-start.3) | async-done | bytes 139296 | tf_op jit(solution)/shard_map/all_to_all | solution.py:56
  143.0 1.4 collective-permute-start.8
  145.0 1.3 collective-permute-start.20
  146.9 2.9 %collective-permute-done.7 = f32[8,4224]{1,0:T(8,128)S(1)} collective-permute-done((f32[8,4224]{1,0:T(8,128)S(1)}, f32[8,4224]{1,0:T(8,128)S(1)}, u32[]{:S(2)}, u32[]{:S(2)}) %collective-permute-start.7) | collective-permute-done | bytes 135200 | tf_op jit(solution)/shard_map/ppermute | solution.py:68
  149.8 1.3 collective-permute-done.6
  151.3 1.5 collective-permute-start.10
  153.4 2.6 %collective-permute-start.24 = (f32[32,4224]{1,0:T(8,128)S(1)}, f32[32,4224]{1,0:T(8,128)}, u32[]{:S(2)}, u32[]{:S(2)}) collective-permute-start(f32[32,4224]{1,0:T(8,128)S(1)} %pad_maximum_fusion.1.refs_6_), channel_id=1, source_target_pairs={{0,192},{64,0},{128,64},{192,128},{1,193},{65,1},{129,65},{193,129... | collective-permute-start | bytes 1622024 | tf_op jit(solution)/shard_map/ppermute | solution.py:75
  156.1 8.0 %collective-permute-start.9 = (f32[32,4224]{1,0:T(8,128)S(1)}, f32[32,4224]{1,0:T(8,128)S(1)}, u32[]{:S(2)}, u32[]{:S(2)}) collective-permute-start(f32[32,4224]{1,0:T(8,128)S(1)} %pad_maximum_fusion.refs_1_), channel_id=1, source_target_pairs={{0,16},{16,0},{1,17},{17,1},{2,18},{18,2},{3,19},{19,3},{4,20},{20... | collective-permute-start | bytes 1622024 | tf_op jit(solution)/shard_map/ppermute | solution.py:85
  164.0 3.5 %collective-permute-start.21 = (f32[32,4224]{1,0:T(8,128)S(1)}, f32[32,4224]{1,0:T(8,128)S(1)}, u32[]{:S(2)}, u32[]{:S(2)}) collective-permute-start(f32[32,4224]{1,0:T(8,128)S(1)} %pad_maximum_fusion.1.refs_6_), channel_id=1, source_target_pairs={{0,16},{16,0},{1,17},{17,1},{2,18},{18,2},{3,19},{19,3},{4,20},{20... | collective-permute-start | bytes 1622024 | tf_op jit(solution)/shard_map/ppermute | solution.py:85
  168.5 2.7 %collective-permute-start.16 = (f32[16,4224]{1,0:T(8,128)S(1)}, f32[16,4224]{1,0:T(8,128)S(1)}, u32[]{:S(2)}, u32[]{:S(2)}) collective-permute-start(f32[16,4224]{1,0:T(8,128)S(1)} %slice.83), channel_id=1, source_target_pairs={{0,33},{1,0},{32,1},{33,32},{2,35},{3,2},{34,3},{35,34},{4,37},{5,... | collective-permute-start | bytes 811016 | tf_op jit(solution)/shard_map/ppermute | solution.py:83
  173.3 1.8 collective-permute-start.28
  178.2 3.1 %collective-permute-done.14.refs_4_ = f32[16,4224]{1,0:T(8,128)S(1)} collective-permute-done((f32[16,4224]{1,0:T(8,128)S(1)}, f32[16,4224]{1,0:T(8,128)S(1)}, u32[]{:S(2)}, u32[]{:S(2)}) %collective-permute-start.14) | collective-permute-done | bytes 270368 | tf_op jit(solution)/shard_map/ppermute | solution.py:83
  181.3 1.1 collective-permute-start.15
  183.7 2.7 %collective-permute-start.11 = (f32[32,4224]{1,0:T(8,128)}, f32[32,4224]{1,0:T(8,128)}, u32[]{:S(2)}, u32[]{:S(2)}) collective-permute-start(f32[32,4224]{1,0:T(8,128)} %collective-permute-done.10.refs_2_), channel_id=1, source_target_pairs={{0,16},{16,0},{1,17},{17,1},{2,18},{18,2},{3,19},{19,3},{4,20},{20... | collective-permute-start | bytes 1622024 | tf_op jit(solution)/shard_map/ppermute | solution.py:85
  189.7 4.9 %shard_map.186 = (f32[512,2048]{1,0:T(8,128)}, f32[512,2048]{1,0:T(8,128)}, f32[64,512]{1,0:T(8,128)}) custom-call(s32[3]{0:T(128)} %pad_add_fusion.refs_0_, f32[32,4224]{1,0:T(8,128)} %copy-done.17, f32[32,4224]{1,0:T(8,128)} %collective-permute-done.10.refs_2_, f32[32,4224]{1,0:T(8,128)} %collective-permute-done.12.refs_3_, f32[16,4224]{1,0:T(8,128)} %copy-done.23, ...), custom_call_target="tpu_custom_call" | custom-call | tf_op jit(solution)/shard_map/pallas_call | solution.py:133
  194.7 4.9 %shard_map.187 = (f32[512,2048]{1,0:T(8,128)}, f32[512,2048]{1,0:T(8,128)}, f32[64,512]{1,0:T(8,128)}) custom-call(s32[3]{0:T(128)} %pad_add_fusion.refs_0_, f32[32,4224]{1,0:T(8,128)} %copy-done.19, f32[32,4224]{1,0:T(8,128)} %collective-permute-done.11.refs_2_, ...), custom_call_target="tpu_custom_call", output_to_operand_aliasing={{0}: (11, {}), {1}: (12, {}), {2}: (13, {})} | custom-call | tf_op jit(solution)/shard_map/pallas_call | solution.py:133
  200.4 1.5 fusion.26
  (130 shorter events, 22.3 us)
Async XLA Ops:
  0.6 14.2 %copy-start = (bf16[512,2048]{1,0:T(8,128)(2,1)S(1)}, bf16[512,2048]{1,0:T(8,128)(2,1)}, u32[]{:S(2)}) copy-start(bf16[512,2048]{1,0:T(8,128)(2,1)} %param.17) | copy-start | bytes 6291460
  0.7 14.1 %copy-start.29 = (f32[2048]{0:T(1024)S(1)}, f32[2048]{0:T(1024)}, u32[]{:S(2)}) copy-start(f32[2048]{0:T(1024)} %param.18) | copy-start | bytes 24580
  18.0 9.7 %copy-start.15 = (bf16[768,2048]{1,0:T(8,128)(2,1)}, bf16[768,2048]{1,0:T(8,128)(2,1)S(1)}, u32[]{:S(2)}) copy-start(bf16[768,2048]{1,0:T(8,128)(2,1)S(1)} %get-tuple-element.43) | copy-start | bytes 9437188
  19.1 4.8 %copy-start.28 = (bf16[512,2048]{1,0:T(8,128)(2,1)S(1)}, bf16[512,2048]{1,0:T(8,128)(2,1)}, u32[]{:S(2)}) copy-start(bf16[512,2048]{1,0:T(8,128)(2,1)} %param.19) | copy-start | bytes 6291460
  19.1 8.6 %collective-permute-start = (f32[256,2048]{1,0:T(8,128)S(1)}, f32[256,2048]{1,0:T(8,128)S(1)}, u32[]{:S(2)}, u32[]{:S(2)}) collective-permute-start(f32[256,2048]{1,0:T(8,128)S(1)} %convolution_multiply_fusion.2), channel_id=1, source_target_pairs={{0,16},{16,0},{1,17},{17,1},{2,18},{18,2},{3,19},{19,3},{4,20},{20... | collective-permute-start | bytes 6291464 | tf_op jit(solution)/shard_map/ppermute | solution.py:295
  34.8 6.3 %copy-start.27 = (f32[512]{0:T(512)S(1)}, f32[512]{0:T(512)}, u32[]{:S(2)}) copy-start(f32[512]{0:T(512)} %param.21) | copy-start | bytes 6148
  34.8 36.9 %all-to-all-start = ((f32[16,16,2048]{2,1,0:T(8,128)}), f32[16,16,2048]{2,1,0:T(8,128)}, u32[]{:S(2)}, u32[]{:S(2)}) async-start(f32[16,16,2048]{2,1,0:T(8,128)} %bitcast.49), calls=%async_computation | async-start | bytes 4194304 | tf_op jit(solution)/shard_map/all_to_all | solution.py:302
  40.1 5.4 %copy-start.14 = (f32[768,512]{1,0:T(8,128)S(1)}, f32[768,512]{1,0:T(8,128)}, u32[]{:S(2)}) copy-start(f32[768,512]{1,0:T(8,128)} %bitcast_convert_fusion) | copy-start | bytes 4718596
  40.1 5.4 %copy-start.16 = (bf16[768,2048]{1,0:T(8,128)(2,1)S(1)}, bf16[768,2048]{1,0:T(8,128)(2,1)}, u32[]{:S(2)}) copy-start(bf16[768,2048]{1,0:T(8,128)(2,1)} %copy-done.15) | copy-start | bytes 9437188
  40.1 5.4 %copy-start.30 = (f32[512]{0:T(512)S(1)}, f32[512]{0:T(512)}, u32[]{:S(2)}) copy-start(f32[512]{0:T(512)} %param.20) | copy-start | bytes 6148
  40.1 27.9 %collective-permute-start.1 = (f32[256,2048]{1,0:T(8,128)}, f32[256,2048]{1,0:T(8,128)}, u32[]{:S(2)}, u32[]{:S(2)}) collective-permute-start(f32[256,2048]{1,0:T(8,128)} %convolution_multiply_fusion), channel_id=1, source_target_pairs={{0,16},{16,0},{1,17},{17,1},{2,18},{18,2},{3,19},{19,3},{4,20},{20... | collective-permute-start | bytes 6291464 | tf_op jit(solution)/shard_map/ppermute | solution.py:306
  52.9 15.1 %copy-start.13 = (f32[256,2048]{1,0:T(8,128)S(1)}, f32[256,2048]{1,0:T(8,128)}, u32[]{:S(2)}) copy-start(f32[256,2048]{1,0:T(8,128)} %broadcast_multiply_fusion) | copy-start | bytes 6291460
  66.6 1.3 collective-permute-start.2
  71.7 41.2 %all-to-all-start.1 = ((f32[16,16,2176]{2,1,0:T(8,128)}), f32[16,16,2176]{2,1,0:T(8,128)}, u32[]{:S(2)}, u32[]{:S(2)}) async-start(f32[16,16,2176]{2,1,0:T(8,128)} %select_maximum_fusion), calls=%async_computation.1 | async-start | bytes 4456448 | tf_op jit(solution)/shard_map/all_to_all | solution.py:345
  79.8 5.2 %collective-permute-start.3 = (f32[16,2048]{1,0:T(8,128)S(1)}, f32[16,2048]{1,0:T(8,128)S(1)}, u32[]{:S(2)}, u32[]{:S(2)}) collective-permute-start(f32[16,2048]{1,0:T(8,128)S(1)} %reduce_sum.58), channel_id=1, source_target_pairs={{0,2},{2,0},{4,6},{6,4},{8,10},{10,8},{12,14},{14,12},{1,3},{3,1},... | collective-permute-start | bytes 393224 | tf_op jit(solution)/shard_map/ppermute | solution.py:62
  85.0 8.9 %collective-permute-start.4 = (f32[16,2048]{1,0:T(8,128)S(1)}, f32[16,2048]{1,0:T(8,128)S(1)}, u32[]{:S(2)}, u32[]{:S(2)}) collective-permute-start(f32[16,2048]{1,0:T(8,128)S(1)} %add.59), channel_id=1, source_target_pairs={{0,4},{2,6},{4,0},{6,2},{8,12},{10,14},{12,8},{14,10},{1,5},{3,7},... | collective-permute-start | bytes 393224 | tf_op jit(solution)/shard_map/ppermute | solution.py:62
  94.0 9.6 %collective-permute-start.5 = (f32[16,2048]{1,0:T(8,128)S(1)}, f32[16,2048]{1,0:T(8,128)S(1)}, u32[]{:S(2)}, u32[]{:S(2)}) collective-permute-start(f32[16,2048]{1,0:T(8,128)S(1)} %add.60), channel_id=1, source_target_pairs={{0,8},{2,10},{4,12},{6,14},{8,0},{10,2},{12,4},{14,6},{1,9},{3,11}... | collective-permute-start | bytes 393224 | tf_op jit(solution)/shard_map/ppermute | solution.py:62
  131.5 11.3 %all-to-all-start.3 = ((f32[8,2,2176]{2,1,0:T(2,128)}), f32[8,2,2176]{2,1,0:T(2,128)S(1)}, u32[]{:S(2)}, u32[]{:S(2)}) async-start(f32[8,2,2176]{2,1,0:T(2,128)} %broadcast_in_dim.5), calls=%async_computation.3 | async-start | bytes 278528 | tf_op jit(solution)/shard_map/all_to_all | solution.py:56
  143.0 3.9 %collective-permute-start.8 = (f32[8,4224]{1,0:T(8,128)S(1)}, f32[8,4224]{1,0:T(8,128)S(1)}, u32[]{:S(2)}, u32[]{:S(2)}) collective-permute-start(f32[8,4224]{1,0:T(8,128)S(1)} %get-tuple-element.59), channel_id=1, source_target_pairs={{0,192},{64,0},{128,64},{192,128},{1,193},{65,1},{129,65},{193,129... | collective-permute-start | bytes 405512 | tf_op jit(solution)/shard_map/ppermute | solution.py:68
  144.3 5.5 %collective-permute-start.7 = (f32[8,4224]{1,0:T(8,128)S(1)}, f32[8,4224]{1,0:T(8,128)S(1)}, u32[]{:S(2)}, u32[]{:S(2)}) collective-permute-start(f32[8,4224]{1,0:T(8,128)S(1)} %get-tuple-element.59), channel_id=1, source_target_pairs={{0,128},{64,192},{128,0},{192,64},{1,129},{65,193},{129,1},{193,65... | collective-permute-start | bytes 405512 | tf_op jit(solution)/shard_map/ppermute | solution.py:68
  144.7 6.4 %collective-permute-start.6 = (f32[8,4224]{1,0:T(8,128)S(1)}, f32[8,4224]{1,0:T(8,128)S(1)}, u32[]{:S(2)}, u32[]{:S(2)}) collective-permute-start(f32[8,4224]{1,0:T(8,128)S(1)} %get-tuple-element.59), channel_id=1, source_target_pairs={{0,64},{64,128},{128,192},{192,0},{1,65},{65,129},{129,193},{193,1... | collective-permute-start | bytes 405512 | tf_op jit(solution)/shard_map/ppermute | solution.py:68
  145.0 7.7 %collective-permute-start.20 = (f32[8,4224]{1,0:T(8,128)S(1)}, f32[8,4224]{1,0:T(8,128)S(1)}, u32[]{:S(2)}, u32[]{:S(2)}) collective-permute-start(f32[8,4224]{1,0:T(8,128)S(1)} %get-tuple-element.58), channel_id=1, source_target_pairs={{0,33},{1,0},{32,1},{33,32},{2,35},{3,2},{34,3},{35,34},{4,37},{5,... | collective-permute-start | bytes 405512 | tf_op jit(solution)/shard_map/ppermute | solution.py:68
  146.3 6.5 %collective-permute-start.19 = (f32[8,4224]{1,0:T(8,128)S(1)}, f32[8,4224]{1,0:T(8,128)S(1)}, u32[]{:S(2)}, u32[]{:S(2)}) collective-permute-start(f32[8,4224]{1,0:T(8,128)S(1)} %get-tuple-element.58), channel_id=1, source_target_pairs={{0,32},{1,33},{32,0},{33,1},{2,34},{3,35},{34,2},{35,3},{4,36},{5,... | collective-permute-start | bytes 405512 | tf_op jit(solution)/shard_map/ppermute | solution.py:68
  146.9 6.5 %collective-permute-start.18 = (f32[8,4224]{1,0:T(8,128)S(1)}, f32[8,4224]{1,0:T(8,128)S(1)}, u32[]{:S(2)}, u32[]{:S(2)}) collective-permute-start(f32[8,4224]{1,0:T(8,128)S(1)} %get-tuple-element.58), channel_id=1, source_target_pairs={{0,1},{1,32},{32,33},{33,0},{2,3},{3,34},{34,35},{35,2},{4,5},{5,3... | collective-permute-start | bytes 405512 | tf_op jit(solution)/shard_map/ppermute | solution.py:68
  151.2 38.5 %copy-start.17 = (f32[32,4224]{1,0:T(8,128)}, f32[32,4224]{1,0:T(8,128)S(1)}, u32[]{:S(2)}) copy-start(f32[32,4224]{1,0:T(8,128)S(1)} %pad_maximum_fusion.refs_1_) | copy-start | bytes 1622020
  151.2 12.8 %collective-permute-start.12 = (f32[32,4224]{1,0:T(8,128)S(1)}, f32[32,4224]{1,0:T(8,128)}, u32[]{:S(2)}, u32[]{:S(2)}) collective-permute-start(f32[32,4224]{1,0:T(8,128)S(1)} %pad_maximum_fusion.refs_1_), channel_id=1, source_target_pairs={{0,33},{1,0},{32,1},{33,32},{2,35},{3,2},{34,3},{35,34},{4,37},{5,... | collective-permute-start | bytes 1622024 | tf_op jit(solution)/shard_map/ppermute | solution.py:75
  151.3 17.3 %collective-permute-start.10 = (f32[32,4224]{1,0:T(8,128)S(1)}, f32[32,4224]{1,0:T(8,128)}, u32[]{:S(2)}, u32[]{:S(2)}) collective-permute-start(f32[32,4224]{1,0:T(8,128)S(1)} %pad_maximum_fusion.refs_1_), channel_id=1, source_target_pairs={{0,1},{1,32},{32,33},{33,0},{2,3},{3,34},{34,35},{35,2},{4,5},{5,3... | collective-permute-start | bytes 1622024 | tf_op jit(solution)/shard_map/ppermute | solution.py:75
  153.4 36.3 %copy-start.18 = (f32[32,4224]{1,0:T(8,128)}, f32[32,4224]{1,0:T(8,128)S(1)}, u32[]{:S(2)}) copy-start(f32[32,4224]{1,0:T(8,128)S(1)} %pad_maximum_fusion.1.refs_6_) | copy-start | bytes 1622020
  153.4 18.8 %collective-permute-start.24 = (f32[32,4224]{1,0:T(8,128)S(1)}, f32[32,4224]{1,0:T(8,128)}, u32[]{:S(2)}, u32[]{:S(2)}) collective-permute-start(f32[32,4224]{1,0:T(8,128)S(1)} %pad_maximum_fusion.1.refs_6_), channel_id=1, source_target_pairs={{0,192},{64,0},{128,64},{192,128},{1,193},{65,1},{129,65},{193,129... | collective-permute-start | bytes 1622024 | tf_op jit(solution)/shard_map/ppermute | solution.py:75
  156.1 17.2 %collective-permute-start.22 = (f32[32,4224]{1,0:T(8,128)S(1)}, f32[32,4224]{1,0:T(8,128)}, u32[]{:S(2)}, u32[]{:S(2)}) collective-permute-start(f32[32,4224]{1,0:T(8,128)S(1)} %pad_maximum_fusion.1.refs_6_), channel_id=1, source_target_pairs={{0,64},{64,128},{128,192},{192,0},{1,65},{65,129},{129,193},{193,1... | collective-permute-start | bytes 1622024 | tf_op jit(solution)/shard_map/ppermute | solution.py:75
  156.1 20.1 %collective-permute-start.9 = (f32[32,4224]{1,0:T(8,128)S(1)}, f32[32,4224]{1,0:T(8,128)S(1)}, u32[]{:S(2)}, u32[]{:S(2)}) collective-permute-start(f32[32,4224]{1,0:T(8,128)S(1)} %pad_maximum_fusion.refs_1_), channel_id=1, source_target_pairs={{0,16},{16,0},{1,17},{17,1},{2,18},{18,2},{3,19},{19,3},{4,20},{20... | collective-permute-start | bytes 1622024 | tf_op jit(solution)/shard_map/ppermute | solution.py:85
  164.0 18.4 %collective-permute-start.21 = (f32[32,4224]{1,0:T(8,128)S(1)}, f32[32,4224]{1,0:T(8,128)S(1)}, u32[]{:S(2)}, u32[]{:S(2)}) collective-permute-start(f32[32,4224]{1,0:T(8,128)S(1)} %pad_maximum_fusion.1.refs_6_), channel_id=1, source_target_pairs={{0,16},{16,0},{1,17},{17,1},{2,18},{18,2},{3,19},{19,3},{4,20},{20... | collective-permute-start | bytes 1622024 | tf_op jit(solution)/shard_map/ppermute | solution.py:85
  168.5 8.5 %collective-permute-start.16 = (f32[16,4224]{1,0:T(8,128)S(1)}, f32[16,4224]{1,0:T(8,128)S(1)}, u32[]{:S(2)}, u32[]{:S(2)}) collective-permute-start(f32[16,4224]{1,0:T(8,128)S(1)} %slice.83), channel_id=1, source_target_pairs={{0,33},{1,0},{32,1},{33,32},{2,35},{3,2},{34,3},{35,34},{4,37},{5,... | collective-permute-start | bytes 811016 | tf_op jit(solution)/shard_map/ppermute | solution.py:83
  172.2 9.0 %collective-permute-start.14 = (f32[16,4224]{1,0:T(8,128)S(1)}, f32[16,4224]{1,0:T(8,128)S(1)}, u32[]{:S(2)}, u32[]{:S(2)}) collective-permute-start(f32[16,4224]{1,0:T(8,128)S(1)} %slice.82), channel_id=1, source_target_pairs={{0,1},{1,32},{32,33},{33,0},{2,3},{3,34},{34,35},{35,2},{4,5},{5,3... | collective-permute-start | bytes 811016 | tf_op jit(solution)/shard_map/ppermute | solution.py:83
  173.3 9.9 %collective-permute-start.28 = (f32[16,4224]{1,0:T(8,128)S(1)}, f32[16,4224]{1,0:T(8,128)S(1)}, u32[]{:S(2)}, u32[]{:S(2)}) collective-permute-start(f32[16,4224]{1,0:T(8,128)S(1)} %slice.86), channel_id=1, source_target_pairs={{0,192},{64,0},{128,64},{192,128},{1,193},{65,1},{129,65},{193,129... | collective-permute-start | bytes 811016 | tf_op jit(solution)/shard_map/ppermute | solution.py:83
  176.1 6.3 %copy-start.19 = (f32[32,4224]{1,0:T(8,128)}, f32[32,4224]{1,0:T(8,128)S(1)}, u32[]{:S(2)}) copy-start(f32[32,4224]{1,0:T(8,128)S(1)} %collective-permute-done.9.refs_1_) | copy-start | bytes 1622020
  176.1 7.6 %collective-permute-start.26 = (f32[16,4224]{1,0:T(8,128)S(1)}, f32[16,4224]{1,0:T(8,128)}, u32[]{:S(2)}, u32[]{:S(2)}) collective-permute-start(f32[16,4224]{1,0:T(8,128)S(1)} %slice.85), channel_id=1, source_target_pairs={{0,64},{64,128},{128,192},{192,0},{1,65},{65,129},{129,193},{193,1... | collective-permute-start | bytes 811016 | tf_op jit(solution)/shard_map/ppermute | solution.py:83
  177.1 12.6 %copy-start.21 = (f32[16,4224]{1,0:T(8,128)}, f32[16,4224]{1,0:T(8,128)S(1)}, u32[]{:S(2)}) copy-start(f32[16,4224]{1,0:T(8,128)S(1)} %collective-permute-done.16.refs_5_) | copy-start | bytes 811012
  177.1 9.3 %collective-permute-start.17 = (f32[16,4224]{1,0:T(8,128)S(1)}, f32[16,4224]{1,0:T(8,128)S(1)}, u32[]{:S(2)}, u32[]{:S(2)}) collective-permute-start(f32[16,4224]{1,0:T(8,128)S(1)} %collective-permute-done.16.refs_5_), channel_id=1, source_target_pairs={{0,16},{16,0},{1,17},{17,1},{2,18},{18,2},{3,19},{19,3},{4,20},{20... | collective-permute-start | bytes 811016 | tf_op jit(solution)/shard_map/ppermute | solution.py:85
  181.3 5.9 %copy-start.23 = (f32[16,4224]{1,0:T(8,128)}, f32[16,4224]{1,0:T(8,128)S(1)}, u32[]{:S(2)}) copy-start(f32[16,4224]{1,0:T(8,128)S(1)} %collective-permute-done.14.refs_4_) | copy-start | bytes 811012
  181.3 5.9 %collective-permute-start.15 = (f32[16,4224]{1,0:T(8,128)S(1)}, f32[16,4224]{1,0:T(8,128)S(1)}, u32[]{:S(2)}, u32[]{:S(2)}) collective-permute-start(f32[16,4224]{1,0:T(8,128)S(1)} %collective-permute-done.14.refs_4_), channel_id=1, source_target_pairs={{0,16},{16,0},{1,17},{17,1},{2,18},{18,2},{3,19},{19,3},{4,20},{20... | collective-permute-start | bytes 811016 | tf_op jit(solution)/shard_map/ppermute | solution.py:85
  182.4 12.2 %collective-permute-start.13 = (f32[32,4224]{1,0:T(8,128)}, f32[32,4224]{1,0:T(8,128)}, u32[]{:S(2)}, u32[]{:S(2)}) collective-permute-start(f32[32,4224]{1,0:T(8,128)} %collective-permute-done.12.refs_3_), channel_id=1, source_target_pairs={{0,16},{16,0},{1,17},{17,1},{2,18},{18,2},{3,19},{19,3},{4,20},{20... | collective-permute-start | bytes 1622024 | tf_op jit(solution)/shard_map/ppermute | solution.py:85
  183.2 5.1 %copy-start.25 = (f32[16,4224]{1,0:T(8,128)}, f32[16,4224]{1,0:T(8,128)S(1)}, u32[]{:S(2)}) copy-start(f32[16,4224]{1,0:T(8,128)S(1)} %collective-permute-done.28.refs_10_) | copy-start | bytes 811012
  183.2 5.1 %collective-permute-start.29 = (f32[16,4224]{1,0:T(8,128)S(1)}, f32[16,4224]{1,0:T(8,128)S(1)}, u32[]{:S(2)}, u32[]{:S(2)}) collective-permute-start(f32[16,4224]{1,0:T(8,128)S(1)} %collective-permute-done.28.refs_10_), channel_id=1, source_target_pairs={{0,16},{16,0},{1,17},{17,1},{2,18},{18,2},{3,19},{19,3},{4,20},{20... | collective-permute-start | bytes 811016 | tf_op jit(solution)/shard_map/ppermute | solution.py:85
  183.7 10.9 %collective-permute-start.11 = (f32[32,4224]{1,0:T(8,128)}, f32[32,4224]{1,0:T(8,128)}, u32[]{:S(2)}, u32[]{:S(2)}) collective-permute-start(f32[32,4224]{1,0:T(8,128)} %collective-permute-done.10.refs_2_), channel_id=1, source_target_pairs={{0,16},{16,0},{1,17},{17,1},{2,18},{18,2},{3,19},{19,3},{4,20},{20... | collective-permute-start | bytes 1622024 | tf_op jit(solution)/shard_map/ppermute | solution.py:85
  187.1 7.5 %collective-permute-start.25 = (f32[32,4224]{1,0:T(8,128)}, f32[32,4224]{1,0:T(8,128)}, u32[]{:S(2)}, u32[]{:S(2)}) collective-permute-start(f32[32,4224]{1,0:T(8,128)} %collective-permute-done.24.refs_8_), channel_id=1, source_target_pairs={{0,16},{16,0},{1,17},{17,1},{2,18},{18,2},{3,19},{19,3},{4,20},{20... | collective-permute-start | bytes 1622024 | tf_op jit(solution)/shard_map/ppermute | solution.py:85
  187.8 6.8 %collective-permute-start.23 = (f32[32,4224]{1,0:T(8,128)}, f32[32,4224]{1,0:T(8,128)}, u32[]{:S(2)}, u32[]{:S(2)}) collective-permute-start(f32[32,4224]{1,0:T(8,128)} %collective-permute-done.22.refs_7_), channel_id=1, source_target_pairs={{0,16},{16,0},{1,17},{17,1},{2,18},{18,2},{3,19},{19,3},{4,20},{20... | collective-permute-start | bytes 1622024 | tf_op jit(solution)/shard_map/ppermute | solution.py:85
  189.1 5.5 %collective-permute-start.27 = (f32[16,4224]{1,0:T(8,128)}, f32[16,4224]{1,0:T(8,128)}, u32[]{:S(2)}, u32[]{:S(2)}) collective-permute-start(f32[16,4224]{1,0:T(8,128)} %collective-permute-done.26.refs_9_), channel_id=1, source_target_pairs={{0,16},{16,0},{1,17},{17,1},{2,18},{18,2},{3,19},{19,3},{4,20},{20... | collective-permute-start | bytes 811016 | tf_op jit(solution)/shard_map/ppermute | solution.py:85
  (16 other events, 35.1 us)
where the time goes:
time: 205 us; the launch traced here: 204 us
  starting transfers between devices  60 us (29%)
  waiting for transfers between devices  41 us (20%)
  Pallas kernels  32.1 us (16%)
  matrix products  22.4 us (11%)
  local copies, waits for them, and re-layouts  16.3 us (8%)
  blocking collectives  16 us (8%)
  other arithmetic  15 us (7%)
    ppermute x10, starting transfers between devices, gather_rest(): return (out, [lax.ppermute(p, 'c', FLIP) for p in out])  17.1 us
    all_to_all x1, blocking collectives, scatter_z(): moved = lax.all_to_all(piece.reshape(8, 2, width), 'z', 0, 0, tiled=True)  16 us
    pallas_call x1, Pallas kernels, backward(): pl.pallas_call(backward_kernel, out_shape=(jax.ShapeDtypeStruct((16, 48,...  13.6 us
    ppermute x3, waiting for transfers between devices, double_z(): piece = piece + lax.ppermute(piece, 'z', [(i, i ^ step) for i in range(8)])  12.4 us
    ppermute x3, starting transfers between devices, double_z(): piece = piece + lax.ppermute(piece, 'z', [(i, i ^ step) for i in range(8)])  11.4 us
    pallas_call x2, Pallas kernels, call(): pl.pallas_call(lambda *refs: place_kernel(far, *refs), out_shape=shapes,...  9.86 us
    all_to_all x1, waiting for transfers between devices, body(): up_piece = jnp.sum(lax.all_to_all(up_mine, PLANE, 0, 0, tiled=True), axis=0)  9.24 us
    pallas_call x1, Pallas kernels, forward(): pl.pallas_call(forward_kernel, out_shape=(jax.ShapeDtypeStruct((768, 512)...  8.58 us
  transfers between devices with their start and end apart: 33, of which 14 were waited for; matrix products, arithmetic and copies ran while one was open for 13% of the time, Pallas kernels for 9%

commit v1 on v0

--- a/solution.py
+++ b/solution.py
@@ -45,22 +45,13 @@
     )
 
 
-def scatter_z(piece):
-    width = piece.shape[1]
-    moved = lax.all_to_all(piece.reshape(8, 2, width), "z", 0, 0, tiled=True)
-    return jnp.sum(moved, axis=0, keepdims=True)
-
-
-def gather_z(summed):
-    width = summed.shape[2]
-    full = lax.all_to_all(jnp.broadcast_to(summed, (8, 2, width)), "z", 0, 0, tiled=True)
-    return full.reshape(16, width)
-
-
-def double_z(piece):
-    for step in (1, 2, 4):
-        piece = piece + lax.ppermute(piece, "z", [(i, i ^ step) for i in range(8)])
-    return piece
+def sum_z(piece):
+    def from_z(v, k):
+        return lax.ppermute(v, "z", [(i, i ^ k) for i in range(8)])
+
+    piece = piece + from_z(piece, 1)
+    far, near, last = from_z(piece, 4), from_z(piece, 2), from_z(piece, 6)
+    return (piece + far) + (near + last)
 
 
 def gather_near(piece):
@@ -85,37 +76,49 @@
     return out, [lax.ppermute(p, "c", FLIP) for p in out]
 
 
+BLOCKS = ((0, 0, 4), (1, 0, 4), (3, 0, 4), (2, 0, 2), (2, 2, 2))
+
+
 def place_kernel(far, where, *refs):
-    pieces, outs, sem = refs[:10], refs[-4:-1], refs[-1]
+    pieces = refs[:10]
+    rest, outs, (small, sem) = refs[10:-11], refs[-11:-2], refs[-2:]
     core, x, y = where[0], where[1], where[2]
+    copies = []
+
+    def each(part):
+        first, second = (x, y) if part == 0 else (y, x)
+        for k, (s1, low, count) in enumerate(BLOCKS):
+            for s2 in range(low, low + count):
+                yield k, lax.rem(first + 4 - s1, 4), lax.rem(second + 4 - s2, 4), (s2 - low) * 8
+
     half = core if far == 0 else 1 - core
-    copies = []
-
-    def copy(src, dst):
-        copies.append(pltpu.make_async_copy(src, dst, sem.at[len(copies)]))
-
     for part in range(2):
-        first, second = (x, y) if part == 0 else (y, x)
-        for k, (s1, low, count) in enumerate(
-            ((0, 0, 4), (1, 0, 4), (3, 0, 4), (2, 0, 2), (2, 2, 2))
-        ):
-            p1 = lax.rem(first + 4 - s1, 4)
-            for s2 in range(low, low + count):
-                p2 = lax.rem(second + 4 - s2, 4)
-                at = p2 * 4 + p1 if part == 0 else p1 * 4 + p2
-                src = pieces[part * 5 + k].at[pl.ds((s2 - low) * 8, 8), :]
-                row = pl.multiple_of(half * 256 + at * 16 + part * 8, 8)
-                copy(src.at[:, pl.ds(0, 2048)], outs[0].at[pl.ds(row, 8), :])
-                copy(src.at[:, pl.ds(2048, 2048)], outs[1].at[pl.ds(row, 8), :])
-                if part == 0:
-                    row = pl.multiple_of(half * 32 + p1 * 8, 8)
-                    lane = pl.multiple_of(p2 * 128, 128)
-                    copy(
-                        src.at[:, pl.ds(4096, 128)],
-                        outs[2].at[pl.ds(row, 8), pl.ds(lane, 128)],
+        for k, p1, p2, at in each(part):
+            block = p2 * 4 + p1 if part == 0 else p1 * 4 + p2
+            src = pieces[part * 5 + k].at[pl.ds(at, 8), :]
+            row = pl.multiple_of(half * 256 + block * 16 + part * 8, 8)
+            for o in range(2):
+                copies.append(
+                    pltpu.make_async_copy(
+                        src.at[:, pl.ds(o * 2048, 2048)],
+                        outs[o].at[pl.ds(row, 8), :],
+                        sem.at[len(copies)],
                     )
+                )
     for c in copies:
         c.start()
+    if far == 1:
+        for which, group in ((1 - core, pieces), (core, rest)):
+            for k, p1, p2, at in each(0):
+                row = pl.multiple_of(which * 32 + p1 * 8, 8)
+                lane = pl.multiple_of(p2 * 128, 128)
+                small[pl.ds(row, 8), pl.ds(lane, 128)] = group[k][pl.ds(at, 8), pl.ds(4096, 128)]
+        for i in range(7):
+            outs[2][i] = small[i * 7 : i * 7 + 7, :]
+        for i in range(5):
+            outs[3 + i][...] = small[49 + i : 50 + i, :]
+        for i in range(4):
+            outs[8][:, i * 512 : i * 512 + 512] = small[54 + i : 55 + i, :]
     for c in copies:
         c.wait()
 
@@ -125,19 +128,25 @@
     where = jnp.stack([c, x, y]).astype(jnp.int32)
     vmem = pl.BlockSpec(memory_space=pltpu.VMEM)
     anywhere = pl.BlockSpec(memory_space=pl.ANY)
-    shapes = tuple(
-        jax.ShapeDtypeStruct(sh, jnp.float32) for sh in ((512, 2048), (512, 2048), (64, 512))
-    )
+    large = ((512, 2048),) * 2
+    small = ((7, 7, 512),) + ((1, 512),) * 5 + ((1, 2048),)
 
     def call(far, pieces, whole):
+        rest = list(own[:5]) if far else []
+        shapes = large + (small if far else ())
+        kernel = place_kernel
+        if not far:
+            kernel = lambda f, *refs: place_kernel(f, *refs[:-4], *refs[-4:-2], *[None] * 7, *refs[-2:])
         return pl.pallas_call(
-            lambda *refs: place_kernel(far, *refs),
-            out_shape=shapes,
-            in_specs=[pl.BlockSpec(memory_space=pltpu.SMEM)] + [vmem] * 10 + [anywhere] * len(whole),
-            out_specs=(anywhere,) * 3,
-            scratch_shapes=[pltpu.SemaphoreType.DMA((80,))],
-            input_output_aliases={11 + i: i for i in range(len(whole))},
-        )(where, *pieces, *whole)
+            lambda *refs: kernel(far, *refs),
+            out_shape=tuple(jax.ShapeDtypeStruct(sh, jnp.float32) for sh in shapes),
+            in_specs=[pl.BlockSpec(memory_space=pltpu.SMEM)]
+            + [vmem] * (10 + len(rest))
+            + [anywhere] * len(whole),
+            out_specs=(anywhere,) * 2 + (vmem,) * (len(shapes) - 2),
+            scratch_shapes=[pltpu.VMEM((64, 512), jnp.float32), pltpu.SemaphoreType.DMA((64,))],
+            input_output_aliases={11 + len(rest) + i: i for i in range(len(whole))},
+        )(where, *pieces, *rest, *whole)
 
     return call(1, other, call(0, own, ()))
 
@@ -152,8 +161,9 @@
                 jnp.float32
             )
 
-    for b in range(4):
-        lanes = slice(b * 128, b * 128 + 128)
+    @pl.loop(0, 4)
+    def _(b):
+        lanes = pl.ds(pl.multiple_of(b * 128, 128), 128)
 
         @pl.loop(0, 4)
         def _(group):
@@ -222,8 +232,9 @@
             sums[2, :, b * 128 : b * 128 + 128] += fold(gm)
             pad[b, h + 3, pl.ds(8, 48), :] = gm
 
-    for b in range(4):
-        lanes = slice(b * 128, b * 128 + 128)
+    @pl.loop(0, 4)
+    def _(b):
+        lanes = pl.ds(pl.multiple_of(b * 128, 128), 128)
         acc[...] = jnp.zeros_like(acc)
 
         @pl.loop(0, 16)
@@ -278,7 +289,6 @@
 ):
     image = inputs[0]
     row_count, column_count, channel_count = image.shape
-    ksize = conv_kernel.shape[0]
     scale = 1.0 / 256
     gain_row = layer_norm_gain.reshape(1, 512)
     standardized_input, normalized_output, inverse_deviation = forward(
@@ -320,7 +330,9 @@
     )
     grad_inputs = grad_inputs.reshape(1, row_count, column_count, channel_count)
 
-    hidden_b, g_pre_c, upstream, _ = lax.optimization_barrier((hidden, g_pre, upstream, up_keep))
+    hidden_b, g_pre_c, grad_out_b, g_branch_c, _ = lax.optimization_barrier(
+        (hidden, g_pre, grad_out, g_branch, up_keep)
+    )
     g_up_bias = jnp.sum(g_pre_c.astype(jnp.float32), axis=0)
     branch = (
         lax.dot_general(
@@ -328,8 +340,8 @@
         )
         + down_bias
     )
-    g_scale = jnp.sum(upstream * branch, axis=0)
-    g_down_bias = jnp.sum((upstream * layer_scale).astype(jnp.bfloat16).astype(jnp.float32), axis=0)
+    g_scale = jnp.sum(grad_out_b.reshape(768, 512).astype(jnp.float32) * branch, axis=0)
+    g_down_bias = jnp.sum(g_branch_c.astype(jnp.float32), axis=0)
     rows = jnp.concatenate([g_down_bias, g_scale, g_up_bias]).reshape(6, 512) * scale
     block = jnp.concatenate([block, rows, jnp.zeros((6, 512), jnp.float32)], axis=0)
     c = lax.axis_index("c")
@@ -343,24 +355,24 @@
     up_mine, moved, grad_inputs = lax.optimization_barrier((up_mine, moved, grad_inputs))
     down_piece = jnp.sum(moved, axis=0)
     up_piece = jnp.sum(lax.all_to_all(up_mine, PLANE, 0, 0, tiled=True), axis=0)
-    down_full = double_z(down_piece)
+    down_full = sum_z(down_piece)
 
     up_piece, down_full = lax.optimization_barrier((up_piece, down_full))
-    up_full = gather_z(scatter_z(up_piece))
+    up_full = sum_z(up_piece)
     near = gather_near(jnp.concatenate([down_full, up_full], axis=1))
     own, other = gather_rest(near, gather_sides(near))
-    gw_down, gw_up, block = place(own, other)
+    gw_down, gw_up, g_kernel, g_gain, g_shift, g_conv, g_down, g_scale, g_up = place(own, other)
     return (
         grad_inputs,
-        block[:49].reshape(ksize, ksize, channel_count),
-        block[51],
-        block[49],
-        block[50],
+        g_kernel,
+        g_conv.reshape(-1),
+        g_gain.reshape(-1),
+        g_shift.reshape(-1),
         gw_up,
-        block[54:58].reshape(-1),
+        g_up.reshape(-1),
         gw_down,
-        block[52],
-        block[53],
+        g_down.reshape(-1),
+        g_scale.reshape(-1),
     )
 
 

time: 205 us -> 196 us (0.956)
  blocking collectives: 16 us -> 0 us
  waiting for transfers between devices: 41 us -> 55.4 us
  local copies, waits for them, and re-layouts: 16.3 us -> 8.32 us
    ppermute x3 -> x8, waiting for transfers between devices: 12.4 us -> 29.3 us  [from_z(): return lax.ppermute(v, 'z', [(i, i ^ k) for i in range(8)])]
    all_to_all x1 -> x0, blocking collectives: 16 us -> none  [scatter_z(): moved = lax.all_to_all(piece.reshape(8, 2, width), 'z', 0, 0, tiled=True)]
    ppermute x3 -> x8, starting transfers between devices: 11.4 us -> 19.5 us  [from_z(): return lax.ppermute(v, 'z', [(i, i ^ k) for i in range(8)])]
    all_to_all x1 -> x0, waiting for transfers between devices: 7.91 us -> none  [gather_z(): lax.all_to_all(jnp.broadcast_to(summed, (8, 2, width)), 'z', 0, 0, tiled=...]
    ppermute x2, waiting for transfers between devices: 0.01 us -> 4.3 us  [gather_sides(): lax.ppermute(p, ax, RING4[3])]
    all_to_all x1 -> x0, starting transfers between devices: 3.37 us -> none  [gather_z(): lax.all_to_all(jnp.broadcast_to(summed, (8, 2, width)), 'z', 0, 0, tiled=...]
    unnamed x65 -> x62, local copies, waits for them, and re-layouts: 8.36 us -> 5.3 us
    ppermute x2, starting transfers between devices: 4.53 us -> 1.6 us  [gather_rest(): lax.ppermute(above[16:], ax, RING4[3])]
  transfers between devices with their start and end apart: 33 -> 37, of which waited for: 14 -> 16; matrix products, arithmetic and copies ran while one was open for 13% -> 12% of each run, Pallas kernels for 9% -> 10%
where the time goes in v1:
time: 196 us
  starting transfers between devices  60.9 us (31%)
  waiting for transfers between devices  55.4 us (28%)
  Pallas kernels  34.1 us (17%)
  matrix products  22.5 us (11%)
  other arithmetic  13.1 us (7%)
  local copies, waits for them, and re-layouts  8.32 us (4%)
    ppermute x8, waiting for transfers between devices, from_z(): return lax.ppermute(v, 'z', [(i, i ^ k) for i in range(8)])  29.3 us
    ppermute x8, starting transfers between devices, from_z(): return lax.ppermute(v, 'z', [(i, i ^ k) for i in range(8)])  19.5 us
    ppermute x10, starting transfers between devices, gather_rest(): return (out, [lax.ppermute(p, 'c', FLIP) for p in out])  14.5 us
    pallas_call x1, Pallas kernels, backward(): pl.pallas_call(backward_kernel, out_shape=(jax.ShapeDtypeStruct((16, 48,...  14.3 us
    pallas_call x2, Pallas kernels, call(): pl.pallas_call(lambda *refs: kernel(far, *refs), out_shape=tuple((jax.Sha...  10.8 us
    all_to_all x1, waiting for transfers between devices, body(): up_piece = jnp.sum(lax.all_to_all(up_mine, PLANE, 0, 0, tiled=True), axis=0)  9.74 us
    pallas_call x1, Pallas kernels, forward(): pl.pallas_call(forward_kernel, out_shape=(jax.ShapeDtypeStruct((768, 512)...  8.94 us
    dot_general x4, matrix products, contract(): lax.dot_general(left, right, (((0,), (0,)), ((), ())), preferred_element_...  8.19 us
  transfers between devices with their start and end apart: 37, of which 16 were waited for; matrix products, arithmetic and copies ran while one was open for 12% of the time, Pallas kernels for 10%

profile of v1, /device:TPU:1, one launch (start us, length us, event | category | flops | bytes accessed | tf_op | source)
XLA Modules:
  0.0 195.7 jit_solution(12911336938716658251)
XLA Ops:
  0.7 1.4 fusion.8
  2.1 1.4 copy-done.1
  6.5 8.9 %conv_norm.1 = (f32[768,512]{1,0:T(8,128)S(1)}, bf16[768,512]{1,0:T(8,128)(2,1)S(1)}, f32[768,1]{1,0:T(8,128)S(1)}) custom-call(bf16[16,48,512]{2,1,0:T(8,128)(2,1)S(1)} %bitcast.39, f32[7,7,512]{2,1,0:T(8,128)S(1)} %copy-done.6, f32[1,512]{1,0:T(1,128)S(1)} %bitcast.45, f32[1,512]{1,0:T(1,128)S(1)} %bitcast.43, f32[1,512]{1,0:T(1,128)S(1)} %bitcast.46), custom_call_target="tpu_custom_call" | custom-call | tf_op jit(solution)/shard_map/conv_norm/pallas_call | solution.py:194
  15.5 3.2 %multiply_convert_fusion = (bf16[768,2048]{1,0:T(8,128)(2,1)S(1)}, f32[768,2048]{1,0:T(8,128)S(1)}) fusion(f32[2048]{0:T(1024)S(1)} %copy-done.29, bf16[768,512]{1,0:T(8,128)(2,1)S(1)} %get-tuple-element.40, bf16[512,2048]{1,0:T(8,128)(2,1)S(1)} %copy-done), kind=kOutput, calls=%fused_computation.8 | convolution fusion | flops 1620049920 | bytes 12328960 | tf_op jit(solution)/shard_map/dot_general | solution.py:297
  19.7 3.3 %collective-permute-start = (f32[256,2048]{1,0:T(8,128)S(1)}, f32[256,2048]{1,0:T(8,128)S(1)}, u32[]{:S(2)}, u32[]{:S(2)}) collective-permute-start(f32[256,2048]{1,0:T(8,128)S(1)} %convolution_multiply_fusion.2), channel_id=1, source_target_pairs={{0,16},{16,0},{1,17},{17,1},{2,18},{18,2},{3,19},{19,3},{4,20},{20... | collective-permute-start | bytes 6291464 | tf_op jit(solution)/shard_map/ppermute | solution.py:305
  23.1 3.8 %fusion.5 = bf16[768,2048]{1,0:T(8,128)(2,1)S(1)} fusion(f32[768,2048]{1,0:T(8,128)S(1)} %get-tuple-element.42, bf16[768,512]{1,0:T(8,128)(2,1)S(1)} %fusion.8, bf16[512,2048]{1,0:T(8,128)(2,1)S(1)} %copy-done.28), kind=kOutput, calls=%fused_computation.6 | convolution fusion | flops 1626341376 | bytes 12320768 | tf_op jit(solution)/shard_map/dot_general | solution.py:308
  26.9 2.4 %fusion.6 = f32[256,2048]{1,0:T(8,128)} fusion(f32[256,2048]{1,0:T(8,128)S(1)} %collective-permute-done, bf16[768,2048]{1,0:T(8,128)(2,1)S(1)} %get-tuple-element.50, pred[]{:T(512)S(6)} %eq.2, bf16[768,512]{1,0:T(8,128)(2,1)S(1)} %fusion.8), kind=kOutput, calls=%fused_computation.13 | convolution fusion | flops 806551552 | bytes 8126465 | tf_op jit(solution)/shard_map/dot_general | solution.py:43
  29.3 2.4 %convolution_multiply_fusion = f32[256,2048]{1,0:T(8,128)} fusion(bf16[768,2048]{1,0:T(8,128)(2,1)S(1)} %fusion.5, pred[]{:T(512)S(6)} %eq.2, bf16[768,512]{1,0:T(8,128)(2,1)S(1)} %get-tuple-element.40), kind=kOutput, calls=%fused_computation.11 | convolution fusion | flops 806027264 | bytes 6029313 | tf_op jit(solution)/shard_map/dot_general | solution.py:43
  31.7 2.4 %broadcast_multiply_fusion = f32[256,2048]{1,0:T(8,128)} fusion(bf16[768,2048]{1,0:T(8,128)(2,1)S(1)} %fusion.5, pred[]{:T(512)S(6)} %eq.2, bf16[768,512]{1,0:T(8,128)(2,1)S(1)} %get-tuple-element.40), kind=kOutput, calls=%fused_computation.22 | convolution fusion | flops 805502976 | bytes 6029313 | tf_op jit(solution)/shard_map/dot_general | solution.py:43
  34.1 6.0 %all-to-all-start = ((f32[16,16,2048]{2,1,0:T(8,128)}), f32[16,16,2048]{2,1,0:T(8,128)}, u32[]{:S(2)}, u32[]{:S(2)}) async-start(f32[16,16,2048]{2,1,0:T(8,128)} %bitcast.48), calls=%async_computation | async-start | bytes 4194304 | tf_op jit(solution)/shard_map/all_to_all | solution.py:312
  41.1 1.4 convert_reduce_fusion.1
  42.6 2.4 %convert_reduce_fusion = f32[2048]{0:T(1024)S(1)} fusion(bf16[768,2048]{1,0:T(8,128)(2,1)} %copy-done.12), kind=kLoop, calls=%fused_computation.7 | loop fusion | flops 3143680 | bytes 3153920 | tf_op jit(solution)/shard_map/reduce_sum | solution.py:336
  45.0 3.5 %fusion.7 = f32[512]{0:T(512)S(1)} fusion(bf16[768,512]{1,0:T(8,128)(2,1)S(1)} %bitcast.41, bf16[768,2048]{1,0:T(8,128)(2,1)S(1)} %copy-done.18, bf16[512,2048]{1,0:T(8,128)(2,1)} %param.19, f32[512]{0:T(512)S(1)} %copy-done.30), kind=kOutput, calls=%fused_computation.18 | convolution fusion | flops 1612185088 | bytes 6033408 | tf_op jit(solution)/shard_map/dot_general | solution.py:338
  48.6 3.9 %fusion.28.gn = f32[768,512]{1,0:T(8,128)S(1)} fusion(bf16[768,2048]{1,0:T(8,128)(2,1)} %copy-done.12, bf16[512,2048]{1,0:T(8,128)(2,1)S(1)} %copy-done), kind=kOutput, calls=%fused_computation.55 | convolution fusion | flops 1610612736 | bytes 6815744 | tf_op jit(solution)/shard_map/dot_general | solution.py:319
  52.5 14.3 %conv_back.1 = (bf16[16,48,512]{2,1,0:T(8,128)(2,1)}, f32[52,512]{1,0:T(8,128)S(1)}) custom-call(f32[768,512]{1,0:T(8,128)S(1)} %fusion.28.gn, f32[768,512]{1,0:T(8,128)S(1)} %copy-done.5, f32[768,1]{1,0:T(8,128)S(1)} %get-tuple-element.46.inv, f32[1,512]{1,0:T(1,128)S(1)} %bitcast.44, bf16[16,48,512]{2,1,0:T(8,128)(2,1)S(1)} %bitcast.40, ...), custom_call_target="tpu_custom_call" | custom-call | flops 80000000 | bytes 6000000 | tf_op jit(solution)/shard_map/conv_back/pallas_call | solution.py:260
  68.4 1.9 multiply_add_fusion
  70.3 1.5 select_maximum_fusion
  71.9 6.8 %all-to-all-start.1 = ((f32[16,16,2176]{2,1,0:T(8,128)}), f32[16,16,2176]{2,1,0:T(8,128)}, u32[]{:S(2)}, u32[]{:S(2)}) async-start(f32[16,16,2176]{2,1,0:T(8,128)} %select_maximum_fusion), calls=%async_computation.1 | async-start | bytes 4456448 | tf_op jit(solution)/shard_map/all_to_all | solution.py:357
  78.7 1.7 reduce_sum.49
  80.4 1.7 collective-permute-start.3
  82.1 3.4 %collective-permute-done.3 = f32[16,2048]{1,0:T(8,128)S(1)} collective-permute-done((f32[16,2048]{1,0:T(8,128)S(1)}, f32[16,2048]{1,0:T(8,128)S(1)}, u32[]{:S(2)}, u32[]{:S(2)}) %collective-permute-start.3) | collective-permute-done | bytes 131104 | tf_op jit(solution)/shard_map/ppermute | solution.py:50
  85.6 5.8 %collective-permute-start.6 = (f32[16,2048]{1,0:T(8,128)S(1)}, f32[16,2048]{1,0:T(8,128)S(1)}, u32[]{:S(2)}, u32[]{:S(2)}) collective-permute-start(f32[16,2048]{1,0:T(8,128)S(1)} %add.74), channel_id=1, source_target_pairs={{0,12},{2,14},{4,8},{6,10},{8,4},{10,6},{12,0},{14,2},{1,13},{3,15... | collective-permute-start | bytes 393224 | tf_op jit(solution)/shard_map/ppermute | solution.py:50
  93.5 3.6 %collective-permute-done.6 = f32[16,2048]{1,0:T(8,128)S(1)} collective-permute-done((f32[16,2048]{1,0:T(8,128)S(1)}, f32[16,2048]{1,0:T(8,128)S(1)}, u32[]{:S(2)}, u32[]{:S(2)}) %collective-permute-start.6) | collective-permute-done | bytes 131104 | tf_op jit(solution)/shard_map/ppermute | solution.py:50
  97.1 1.3 collective-permute-done.5
  98.4 5.2 %collective-permute-done.4 = f32[16,2048]{1,0:T(8,128)S(1)} collective-permute-done((f32[16,2048]{1,0:T(8,128)S(1)}, f32[16,2048]{1,0:T(8,128)S(1)}, u32[]{:S(2)}, u32[]{:S(2)}) %collective-permute-start.4) | collective-permute-done | bytes 131104 | tf_op jit(solution)/shard_map/ppermute | solution.py:50
  103.7 9.7 %all-to-all-done.1 = f32[16,16,2176]{2,1,0:T(8,128)} async-done(((f32[16,16,2176]{2,1,0:T(8,128)}), f32[16,16,2176]{2,1,0:T(8,128)}, u32[]{:S(2)}, u32[]{:S(2)}) %all-to-all-start.1) | async-done | bytes 2228256 | tf_op jit(solution)/shard_map/all_to_all | solution.py:357
  113.4 1.7 reduce_sum.48
  115.1 1.7 collective-permute-start.7
  116.9 2.4 %collective-permute-done.7 = f32[16,2176]{1,0:T(8,128)S(1)} collective-permute-done((f32[16,2176]{1,0:T(8,128)S(1)}, f32[16,2176]{1,0:T(8,128)S(1)}, u32[]{:S(2)}, u32[]{:S(2)}) %collective-permute-start.7) | collective-permute-done | bytes 139296 | tf_op jit(solution)/shard_map/ppermute | solution.py:50
  119.3 5.9 %collective-permute-start.10 = (f32[16,2176]{1,0:T(8,128)S(1)}, f32[16,2176]{1,0:T(8,128)S(1)}, u32[]{:S(2)}, u32[]{:S(2)}) collective-permute-start(f32[16,2176]{1,0:T(8,128)S(1)} %add.78), channel_id=1, source_target_pairs={{0,12},{2,14},{4,8},{6,10},{8,4},{10,6},{12,0},{14,2},{1,13},{3,15... | collective-permute-start | bytes 417800 | tf_op jit(solution)/shard_map/ppermute | solution.py:50
  127.5 2.1 %collective-permute-done.10 = f32[16,2176]{1,0:T(8,128)S(1)} collective-permute-done((f32[16,2176]{1,0:T(8,128)S(1)}, f32[16,2176]{1,0:T(8,128)S(1)}, u32[]{:S(2)}, u32[]{:S(2)}) %collective-permute-start.10) | collective-permute-done | bytes 139296 | tf_op jit(solution)/shard_map/ppermute | solution.py:50
  129.5 1.3 collective-permute-done.9
  130.9 9.9 %collective-permute-done.8 = f32[16,2176]{1,0:T(8,128)S(1)} collective-permute-done((f32[16,2176]{1,0:T(8,128)S(1)}, f32[16,2176]{1,0:T(8,128)S(1)}, u32[]{:S(2)}, u32[]{:S(2)}) %collective-permute-start.8) | collective-permute-done | bytes 139296 | tf_op jit(solution)/shard_map/ppermute | solution.py:50
  140.8 1.4 collective-permute-start.13
  142.9 1.2 collective-permute-start.25
  144.8 2.9 %collective-permute-done.12 = f32[8,4224]{1,0:T(8,128)S(1)} collective-permute-done((f32[8,4224]{1,0:T(8,128)S(1)}, f32[8,4224]{1,0:T(8,128)S(1)}, u32[]{:S(2)}, u32[]{:S(2)}) %collective-permute-start.12) | collective-permute-done | bytes 135200 | tf_op jit(solution)/shard_map/ppermute | solution.py:59
  147.7 3.9 %collective-permute-done.11 = f32[8,4224]{1,0:T(8,128)S(1)} collective-permute-done((f32[8,4224]{1,0:T(8,128)S(1)}, f32[8,4224]{1,0:T(8,128)S(1)}, u32[]{:S(2)}, u32[]{:S(2)}) %collective-permute-start.11) | collective-permute-done | bytes 135200 | tf_op jit(solution)/shard_map/ppermute | solution.py:59
  151.8 1.5 collective-permute-start.15
  154.8 5.6 %collective-permute-start.14 = (f32[32,4224]{1,0:T(8,128)S(1)}, f32[32,4224]{1,0:T(8,128)S(1)}, u32[]{:S(2)}, u32[]{:S(2)}) collective-permute-start(f32[32,4224]{1,0:T(8,128)S(1)} %pad_maximum_fusion.refs_1_.refs_11_), channel_id=1, source_target_pairs={{0,16},{16,0},{1,17},{17,1},{2,18},{18,2},{3,19},{19,3},{4,20},{20... | collective-permute-start | bytes 1622024 | tf_op jit(solution)/shard_map/ppermute | solution.py:76
  160.4 4.3 %collective-permute-done.17.refs_3_.refs_13_ = f32[32,4224]{1,0:T(8,128)S(1)} collective-permute-done((f32[32,4224]{1,0:T(8,128)S(1)}, f32[32,4224]{1,0:T(8,128)S(1)}, u32[]{:S(2)}, u32[]{:S(2)}) %collective-permute-start.17) | collective-permute-done | bytes 540704 | tf_op jit(solution)/shard_map/ppermute | solution.py:66
  164.7 1.7 collective-permute-start.26
  166.5 1.3 collective-permute-start.21
  171.4 1.3 collective-permute-start.31
  173.6 1.8 collective-permute-start.22
  175.5 2.3 %collective-permute-done.19.refs_4_.refs_14_ = f32[16,4224]{1,0:T(8,128)S(1)} collective-permute-done((f32[16,4224]{1,0:T(8,128)S(1)}, f32[16,4224]{1,0:T(8,128)S(1)}, u32[]{:S(2)}, u32[]{:S(2)}) %collective-permute-start.19) | collective-permute-done | bytes 270368 | tf_op jit(solution)/shard_map/ppermute | solution.py:74
  179.6 2.5 %collective-permute-start.16 = (f32[32,4224]{1,0:T(8,128)}, f32[32,4224]{1,0:T(8,128)}, u32[]{:S(2)}, u32[]{:S(2)}) collective-permute-start(f32[32,4224]{1,0:T(8,128)} %collective-permute-done.15.refs_2_.refs_12_), channel_id=1, source_target_pairs={{0,16},{16,0},{1,17},{17,1},{2,18},{18,2},{3,19},{19,3},{4,20},{20... | collective-permute-start | bytes 1622024 | tf_op jit(solution)/shard_map/ppermute | solution.py:76
  184.6 4.7 %shard_map.186 = (f32[512,2048]{1,0:T(8,128)}, f32[512,2048]{1,0:T(8,128)}) custom-call(s32[3]{0:T(128)} %pad_add_fusion.refs_0_, f32[32,4224]{1,0:T(8,128)} %copy-done.15, f32[32,4224]{1,0:T(8,128)} %collective-permute-done.15.refs_2_.refs_12_, f32[32,4224]{1,0:T(8,128)} %copy-done.16, f32[16,4224]{1,0:T(8,128)} %copy-done.21, f32[16,4224]{1,0:T(8,128)} %copy-done.20, ...), custom_call_target="tpu_custom_call" | custom-call | tf_op jit(solution)/shard_map/pallas_call | solution.py:140
  189.4 6.1 %shard_map.187 = (f32[512,2048]{1,0:T(8,128)}, f32[512,2048]{1,0:T(8,128)}, f32[7,7,512]{2,1,0:T(8,128)}, f32[1,512]{1,0:T(1,128)}, f32[1,512]{1,0:T(1,128)}, /*...) custom-call(s32[3]{0:T(128)} %pad_add_fusion.refs_0_, ...), custom_call_target="tpu_custom_call", output_to_operand_aliasing={{0}: (16, {}), {1}: (17, {})} | custom-call | tf_op jit(solution)/shard_map/pallas_call | solution.py:140
  (126 shorter events, 23.2 us)
Async XLA Ops:
  0.6 14.8 %copy-start = (bf16[512,2048]{1,0:T(8,128)(2,1)S(1)}, bf16[512,2048]{1,0:T(8,128)(2,1)}, u32[]{:S(2)}) copy-start(bf16[512,2048]{1,0:T(8,128)(2,1)} %param.17) | copy-start | bytes 6291460
  0.7 14.8 %copy-start.29 = (f32[2048]{0:T(1024)S(1)}, f32[2048]{0:T(1024)}, u32[]{:S(2)}) copy-start(f32[2048]{0:T(1024)} %param.18) | copy-start | bytes 24580
  2.1 24.8 %copy-start.14 = (bf16[768,512]{1,0:T(8,128)(2,1)}, bf16[768,512]{1,0:T(8,128)(2,1)S(1)}, u32[]{:S(2)}) copy-start(bf16[768,512]{1,0:T(8,128)(2,1)S(1)} %fusion.8) | copy-start | bytes 2359300
  18.6 8.3 %copy-start.17 = (bf16[768,2048]{1,0:T(8,128)(2,1)}, bf16[768,2048]{1,0:T(8,128)(2,1)S(1)}, u32[]{:S(2)}) copy-start(bf16[768,2048]{1,0:T(8,128)(2,1)S(1)} %get-tuple-element.50) | copy-start | bytes 9437188
  19.7 7.2 %collective-permute-start = (f32[256,2048]{1,0:T(8,128)S(1)}, f32[256,2048]{1,0:T(8,128)S(1)}, u32[]{:S(2)}, u32[]{:S(2)}) collective-permute-start(f32[256,2048]{1,0:T(8,128)S(1)} %convolution_multiply_fusion.2), channel_id=1, source_target_pairs={{0,16},{16,0},{1,17},{17,1},{2,18},{18,2},{3,19},{19,3},{4,20},{20... | collective-permute-start | bytes 6291464 | tf_op jit(solution)/shard_map/ppermute | solution.py:305
  34.1 37.8 %all-to-all-start = ((f32[16,16,2048]{2,1,0:T(8,128)}), f32[16,16,2048]{2,1,0:T(8,128)}, u32[]{:S(2)}, u32[]{:S(2)}) async-start(f32[16,16,2048]{2,1,0:T(8,128)} %bitcast.48), calls=%async_computation | async-start | bytes 4194304 | tf_op jit(solution)/shard_map/all_to_all | solution.py:312
  40.1 4.9 %copy-start.3 = (bf16[1,16,48,512]{3,2,1,0:T(8,128)(2,1)S(1)}, bf16[1,16,48,512]{3,2,1,0:T(8,128)(2,1)}, u32[]{:S(2)}) copy-start(bf16[1,16,48,512]{3,2,1,0:T(8,128)(2,1)} %param.12) | copy-start | bytes 2359300
  40.1 28.3 %collective-permute-start.1 = (f32[256,2048]{1,0:T(8,128)}, f32[256,2048]{1,0:T(8,128)}, u32[]{:S(2)}, u32[]{:S(2)}) collective-permute-start(f32[256,2048]{1,0:T(8,128)} %convolution_multiply_fusion), channel_id=1, source_target_pairs={{0,16},{16,0},{1,17},{17,1},{2,18},{18,2},{3,19},{19,3},{4,20},{20... | collective-permute-start | bytes 6291464 | tf_op jit(solution)/shard_map/ppermute | solution.py:316
  52.5 16.0 %copy-start.13 = (f32[256,2048]{1,0:T(8,128)S(1)}, f32[256,2048]{1,0:T(8,128)}, u32[]{:S(2)}) copy-start(f32[256,2048]{1,0:T(8,128)} %broadcast_multiply_fusion) | copy-start | bytes 6291460
  66.9 1.5 collective-permute-start.2
  71.9 41.5 %all-to-all-start.1 = ((f32[16,16,2176]{2,1,0:T(8,128)}), f32[16,16,2176]{2,1,0:T(8,128)}, u32[]{:S(2)}, u32[]{:S(2)}) async-start(f32[16,16,2176]{2,1,0:T(8,128)} %select_maximum_fusion), calls=%async_computation.1 | async-start | bytes 4456448 | tf_op jit(solution)/shard_map/all_to_all | solution.py:357
  80.4 5.1 %collective-permute-start.3 = (f32[16,2048]{1,0:T(8,128)S(1)}, f32[16,2048]{1,0:T(8,128)S(1)}, u32[]{:S(2)}, u32[]{:S(2)}) collective-permute-start(f32[16,2048]{1,0:T(8,128)S(1)} %reduce_sum.49), channel_id=1, source_target_pairs={{0,2},{2,0},{4,6},{6,4},{8,10},{10,8},{12,14},{14,12},{1,3},{3,1},... | collective-permute-start | bytes 393224 | tf_op jit(solution)/shard_map/ppermute | solution.py:50
  85.6 11.6 %collective-permute-start.6 = (f32[16,2048]{1,0:T(8,128)S(1)}, f32[16,2048]{1,0:T(8,128)S(1)}, u32[]{:S(2)}, u32[]{:S(2)}) collective-permute-start(f32[16,2048]{1,0:T(8,128)S(1)} %add.74), channel_id=1, source_target_pairs={{0,12},{2,14},{4,8},{6,10},{8,4},{10,6},{12,0},{14,2},{1,13},{3,15... | collective-permute-start | bytes 393224 | tf_op jit(solution)/shard_map/ppermute | solution.py:50
  91.3 7.1 %collective-permute-start.5 = (f32[16,2048]{1,0:T(8,128)S(1)}, f32[16,2048]{1,0:T(8,128)S(1)}, u32[]{:S(2)}, u32[]{:S(2)}) collective-permute-start(f32[16,2048]{1,0:T(8,128)S(1)} %add.74), channel_id=1, source_target_pairs={{0,4},{2,6},{4,0},{6,2},{8,12},{10,14},{12,8},{14,10},{1,5},{3,7},... | collective-permute-start | bytes 393224 | tf_op jit(solution)/shard_map/ppermute | solution.py:50
  92.5 11.1 %collective-permute-start.4 = (f32[16,2048]{1,0:T(8,128)S(1)}, f32[16,2048]{1,0:T(8,128)S(1)}, u32[]{:S(2)}, u32[]{:S(2)}) collective-permute-start(f32[16,2048]{1,0:T(8,128)S(1)} %add.74), channel_id=1, source_target_pairs={{0,8},{2,10},{4,12},{6,14},{8,0},{10,2},{12,4},{14,6},{1,9},{3,11}... | collective-permute-start | bytes 393224 | tf_op jit(solution)/shard_map/ppermute | solution.py:50
  115.1 4.2 %collective-permute-start.7 = (f32[16,2176]{1,0:T(8,128)S(1)}, f32[16,2176]{1,0:T(8,128)S(1)}, u32[]{:S(2)}, u32[]{:S(2)}) collective-permute-start(f32[16,2176]{1,0:T(8,128)S(1)} %reduce_sum.48), channel_id=1, source_target_pairs={{0,2},{2,0},{4,6},{6,4},{8,10},{10,8},{12,14},{14,12},{1,3},{3,1},... | collective-permute-start | bytes 417800 | tf_op jit(solution)/shard_map/ppermute | solution.py:50
  119.3 10.2 %collective-permute-start.10 = (f32[16,2176]{1,0:T(8,128)S(1)}, f32[16,2176]{1,0:T(8,128)S(1)}, u32[]{:S(2)}, u32[]{:S(2)}) collective-permute-start(f32[16,2176]{1,0:T(8,128)S(1)} %add.78), channel_id=1, source_target_pairs={{0,12},{2,14},{4,8},{6,10},{8,4},{10,6},{12,0},{14,2},{1,13},{3,15... | collective-permute-start | bytes 417800 | tf_op jit(solution)/shard_map/ppermute | solution.py:50
  125.3 5.6 %collective-permute-start.9 = (f32[16,2176]{1,0:T(8,128)S(1)}, f32[16,2176]{1,0:T(8,128)S(1)}, u32[]{:S(2)}, u32[]{:S(2)}) collective-permute-start(f32[16,2176]{1,0:T(8,128)S(1)} %add.78), channel_id=1, source_target_pairs={{0,4},{2,6},{4,0},{6,2},{8,12},{10,14},{12,8},{14,10},{1,5},{3,7},... | collective-permute-start | bytes 417800 | tf_op jit(solution)/shard_map/ppermute | solution.py:50
  126.4 14.3 %collective-permute-start.8 = (f32[16,2176]{1,0:T(8,128)S(1)}, f32[16,2176]{1,0:T(8,128)S(1)}, u32[]{:S(2)}, u32[]{:S(2)}) collective-permute-start(f32[16,2176]{1,0:T(8,128)S(1)} %add.78), channel_id=1, source_target_pairs={{0,8},{2,10},{4,12},{6,14},{8,0},{10,2},{12,4},{14,6},{1,9},{3,11}... | collective-permute-start | bytes 417800 | tf_op jit(solution)/shard_map/ppermute | solution.py:50
  140.8 3.9 %collective-permute-start.13 = (f32[8,4224]{1,0:T(8,128)S(1)}, f32[8,4224]{1,0:T(8,128)S(1)}, u32[]{:S(2)}, u32[]{:S(2)}) collective-permute-start(f32[8,4224]{1,0:T(8,128)S(1)} %get-tuple-element.71), channel_id=1, source_target_pairs={{0,192},{64,0},{128,64},{192,128},{1,193},{65,1},{129,65},{193,129... | collective-permute-start | bytes 405512 | tf_op jit(solution)/shard_map/ppermute | solution.py:59
  142.2 5.5 %collective-permute-start.12 = (f32[8,4224]{1,0:T(8,128)S(1)}, f32[8,4224]{1,0:T(8,128)S(1)}, u32[]{:S(2)}, u32[]{:S(2)}) collective-permute-start(f32[8,4224]{1,0:T(8,128)S(1)} %get-tuple-element.71), channel_id=1, source_target_pairs={{0,128},{64,192},{128,0},{192,64},{1,129},{65,193},{129,1},{193,65... | collective-permute-start | bytes 405512 | tf_op jit(solution)/shard_map/ppermute | solution.py:59
  142.6 9.0 %collective-permute-start.11 = (f32[8,4224]{1,0:T(8,128)S(1)}, f32[8,4224]{1,0:T(8,128)S(1)}, u32[]{:S(2)}, u32[]{:S(2)}) collective-permute-start(f32[8,4224]{1,0:T(8,128)S(1)} %get-tuple-element.71), channel_id=1, source_target_pairs={{0,64},{64,128},{128,192},{192,0},{1,65},{65,129},{129,193},{193,1... | collective-permute-start | bytes 405512 | tf_op jit(solution)/shard_map/ppermute | solution.py:59
  142.9 10.3 %collective-permute-start.25 = (f32[8,4224]{1,0:T(8,128)S(1)}, f32[8,4224]{1,0:T(8,128)S(1)}, u32[]{:S(2)}, u32[]{:S(2)}) collective-permute-start(f32[8,4224]{1,0:T(8,128)S(1)} %get-tuple-element.70), channel_id=1, source_target_pairs={{0,33},{1,0},{32,1},{33,32},{2,35},{3,2},{34,3},{35,34},{4,37},{5,... | collective-permute-start | bytes 405512 | tf_op jit(solution)/shard_map/ppermute | solution.py:59
  144.1 9.1 %collective-permute-start.24 = (f32[8,4224]{1,0:T(8,128)S(1)}, f32[8,4224]{1,0:T(8,128)S(1)}, u32[]{:S(2)}, u32[]{:S(2)}) collective-permute-start(f32[8,4224]{1,0:T(8,128)S(1)} %get-tuple-element.70), channel_id=1, source_target_pairs={{0,32},{1,33},{32,0},{33,1},{2,34},{3,35},{34,2},{35,3},{4,36},{5,... | collective-permute-start | bytes 405512 | tf_op jit(solution)/shard_map/ppermute | solution.py:59
  144.8 8.4 %collective-permute-start.23 = (f32[8,4224]{1,0:T(8,128)S(1)}, f32[8,4224]{1,0:T(8,128)S(1)}, u32[]{:S(2)}, u32[]{:S(2)}) collective-permute-start(f32[8,4224]{1,0:T(8,128)S(1)} %get-tuple-element.70), channel_id=1, source_target_pairs={{0,1},{1,32},{32,33},{33,0},{2,3},{3,34},{34,35},{35,2},{4,5},{5,3... | collective-permute-start | bytes 405512 | tf_op jit(solution)/shard_map/ppermute | solution.py:59
  151.7 33.0 %copy-start.15 = (f32[32,4224]{1,0:T(8,128)}, f32[32,4224]{1,0:T(8,128)S(1)}, u32[]{:S(2)}) copy-start(f32[32,4224]{1,0:T(8,128)S(1)} %pad_maximum_fusion.refs_1_.refs_11_) | copy-start | bytes 1622020
  151.7 13.0 %collective-permute-start.17 = (f32[32,4224]{1,0:T(8,128)S(1)}, f32[32,4224]{1,0:T(8,128)S(1)}, u32[]{:S(2)}, u32[]{:S(2)}) collective-permute-start(f32[32,4224]{1,0:T(8,128)S(1)} %pad_maximum_fusion.refs_1_.refs_11_), channel_id=1, source_target_pairs={{0,33},{1,0},{32,1},{33,32},{2,35},{3,2},{34,3},{35,34},{4,37},{5,... | collective-permute-start | bytes 1622024 | tf_op jit(solution)/shard_map/ppermute | solution.py:66
  151.8 14.7 %collective-permute-start.15 = (f32[32,4224]{1,0:T(8,128)S(1)}, f32[32,4224]{1,0:T(8,128)}, u32[]{:S(2)}, u32[]{:S(2)}) collective-permute-start(f32[32,4224]{1,0:T(8,128)S(1)} %pad_maximum_fusion.refs_1_.refs_11_), channel_id=1, source_target_pairs={{0,1},{1,32},{32,33},{33,0},{2,3},{3,34},{34,35},{35,2},{4,5},{5,3... | collective-permute-start | bytes 1622024 | tf_op jit(solution)/shard_map/ppermute | solution.py:66
  153.3 25.7 %copy-start.19 = (f32[32,4224]{1,0:T(8,128)}, f32[32,4224]{1,0:T(8,128)S(1)}, u32[]{:S(2)}) copy-start(f32[32,4224]{1,0:T(8,128)S(1)} %pad_maximum_fusion.1.refs_6_) | copy-start | bytes 1622020
  153.3 15.5 %collective-permute-start.29 = (f32[32,4224]{1,0:T(8,128)S(1)}, f32[32,4224]{1,0:T(8,128)}, u32[]{:S(2)}, u32[]{:S(2)}) collective-permute-start(f32[32,4224]{1,0:T(8,128)S(1)} %pad_maximum_fusion.1.refs_6_), channel_id=1, source_target_pairs={{0,192},{64,0},{128,64},{192,128},{1,193},{65,1},{129,65},{193,129... | collective-permute-start | bytes 1622024 | tf_op jit(solution)/shard_map/ppermute | solution.py:66
  153.8 16.3 %collective-permute-start.27 = (f32[32,4224]{1,0:T(8,128)S(1)}, f32[32,4224]{1,0:T(8,128)}, u32[]{:S(2)}, u32[]{:S(2)}) collective-permute-start(f32[32,4224]{1,0:T(8,128)S(1)} %pad_maximum_fusion.1.refs_6_), channel_id=1, source_target_pairs={{0,64},{64,128},{128,192},{192,0},{1,65},{65,129},{129,193},{193,1... | collective-permute-start | bytes 1622024 | tf_op jit(solution)/shard_map/ppermute | solution.py:66
  154.8 16.5 %collective-permute-start.14 = (f32[32,4224]{1,0:T(8,128)S(1)}, f32[32,4224]{1,0:T(8,128)S(1)}, u32[]{:S(2)}, u32[]{:S(2)}) collective-permute-start(f32[32,4224]{1,0:T(8,128)S(1)} %pad_maximum_fusion.refs_1_.refs_11_), channel_id=1, source_target_pairs={{0,16},{16,0},{1,17},{17,1},{2,18},{18,2},{3,19},{19,3},{4,20},{20... | collective-permute-start | bytes 1622024 | tf_op jit(solution)/shard_map/ppermute | solution.py:76
  164.7 19.9 %copy-start.16 = (f32[32,4224]{1,0:T(8,128)}, f32[32,4224]{1,0:T(8,128)S(1)}, u32[]{:S(2)}) copy-start(f32[32,4224]{1,0:T(8,128)S(1)} %collective-permute-done.17.refs_3_.refs_13_) | copy-start | bytes 1622020
  164.7 14.2 %collective-permute-start.26 = (f32[32,4224]{1,0:T(8,128)S(1)}, f32[32,4224]{1,0:T(8,128)S(1)}, u32[]{:S(2)}, u32[]{:S(2)}) collective-permute-start(f32[32,4224]{1,0:T(8,128)S(1)} %pad_maximum_fusion.1.refs_6_), channel_id=1, source_target_pairs={{0,16},{16,0},{1,17},{17,1},{2,18},{18,2},{3,19},{19,3},{4,20},{20... | collective-permute-start | bytes 1622024 | tf_op jit(solution)/shard_map/ppermute | solution.py:76
  166.5 7.1 %collective-permute-start.21 = (f32[16,4224]{1,0:T(8,128)S(1)}, f32[16,4224]{1,0:T(8,128)S(1)}, u32[]{:S(2)}, u32[]{:S(2)}) collective-permute-start(f32[16,4224]{1,0:T(8,128)S(1)} %slice.56), channel_id=1, source_target_pairs={{0,33},{1,0},{32,1},{33,32},{2,35},{3,2},{34,3},{35,34},{4,37},{5,... | collective-permute-start | bytes 811016 | tf_op jit(solution)/shard_map/ppermute | solution.py:74
  168.8 9.0 %collective-permute-start.19 = (f32[16,4224]{1,0:T(8,128)S(1)}, f32[16,4224]{1,0:T(8,128)S(1)}, u32[]{:S(2)}, u32[]{:S(2)}) collective-permute-start(f32[16,4224]{1,0:T(8,128)S(1)} %slice.55), channel_id=1, source_target_pairs={{0,1},{1,32},{32,33},{33,0},{2,3},{3,34},{34,35},{35,2},{4,5},{5,3... | collective-permute-start | bytes 811016 | tf_op jit(solution)/shard_map/ppermute | solution.py:74
  170.1 9.0 %collective-permute-start.33 = (f32[16,4224]{1,0:T(8,128)S(1)}, f32[16,4224]{1,0:T(8,128)S(1)}, u32[]{:S(2)}, u32[]{:S(2)}) collective-permute-start(f32[16,4224]{1,0:T(8,128)S(1)} %slice.58), channel_id=1, source_target_pairs={{0,192},{64,0},{128,64},{192,128},{1,193},{65,1},{129,65},{193,129... | collective-permute-start | bytes 811016 | tf_op jit(solution)/shard_map/ppermute | solution.py:74
  171.4 10.8 %copy-start.22 = (f32[32,4224]{1,0:T(8,128)}, f32[32,4224]{1,0:T(8,128)S(1)}, u32[]{:S(2)}) copy-start(f32[32,4224]{1,0:T(8,128)S(1)} %collective-permute-done.14.refs_1_) | copy-start | bytes 1622020
  171.4 8.2 %collective-permute-start.31 = (f32[16,4224]{1,0:T(8,128)S(1)}, f32[16,4224]{1,0:T(8,128)}, u32[]{:S(2)}, u32[]{:S(2)}) collective-permute-start(f32[16,4224]{1,0:T(8,128)S(1)} %slice.57), channel_id=1, source_target_pairs={{0,64},{64,128},{128,192},{192,0},{1,65},{65,129},{129,193},{193,1... | collective-permute-start | bytes 811016 | tf_op jit(solution)/shard_map/ppermute | solution.py:74
  173.6 11.0 %copy-start.20 = (f32[16,4224]{1,0:T(8,128)}, f32[16,4224]{1,0:T(8,128)S(1)}, u32[]{:S(2)}) copy-start(f32[16,4224]{1,0:T(8,128)S(1)} %collective-permute-done.21.refs_5_.refs_15_) | copy-start | bytes 811012
  173.6 8.4 %collective-permute-start.22 = (f32[16,4224]{1,0:T(8,128)S(1)}, f32[16,4224]{1,0:T(8,128)S(1)}, u32[]{:S(2)}, u32[]{:S(2)}) collective-permute-start(f32[16,4224]{1,0:T(8,128)S(1)} %collective-permute-done.21.refs_5_.refs_15_), channel_id=1, source_target_pairs={{0,16},{16,0},{1,17},{17,1},{2,18},{18,2},{3,19},{19,3},{4,20},{20... | collective-permute-start | bytes 811016 | tf_op jit(solution)/shard_map/ppermute | solution.py:76
  177.8 4.4 %collective-permute-start.20 = (f32[16,4224]{1,0:T(8,128)S(1)}, f32[16,4224]{1,0:T(8,128)S(1)}, u32[]{:S(2)}, u32[]{:S(2)}) collective-permute-start(f32[16,4224]{1,0:T(8,128)S(1)} %collective-permute-done.19.refs_4_.refs_14_), channel_id=1, source_target_pairs={{0,16},{16,0},{1,17},{17,1},{2,18},{18,2},{3,19},{19,3},{4,20},{20... | collective-permute-start | bytes 811016 | tf_op jit(solution)/shard_map/ppermute | solution.py:76
  179.0 10.4 %collective-permute-start.18 = (f32[32,4224]{1,0:T(8,128)S(1)}, f32[32,4224]{1,0:T(8,128)}, u32[]{:S(2)}, u32[]{:S(2)}) collective-permute-start(f32[32,4224]{1,0:T(8,128)S(1)} %collective-permute-done.17.refs_3_.refs_13_), channel_id=1, source_target_pairs={{0,16},{16,0},{1,17},{17,1},{2,18},{18,2},{3,19},{19,3},{4,20},{20... | collective-permute-start | bytes 1622024 | tf_op jit(solution)/shard_map/ppermute | solution.py:76
  179.1 3.7 %collective-permute-start.34 = (f32[16,4224]{1,0:T(8,128)S(1)}, f32[16,4224]{1,0:T(8,128)S(1)}, u32[]{:S(2)}, u32[]{:S(2)}) collective-permute-start(f32[16,4224]{1,0:T(8,128)S(1)} %collective-permute-done.33.refs_10_), channel_id=1, source_target_pairs={{0,16},{16,0},{1,17},{17,1},{2,18},{18,2},{3,19},{19,3},{4,20},{20... | collective-permute-start | bytes 811016 | tf_op jit(solution)/shard_map/ppermute | solution.py:76
  179.6 9.8 %collective-permute-start.16 = (f32[32,4224]{1,0:T(8,128)}, f32[32,4224]{1,0:T(8,128)}, u32[]{:S(2)}, u32[]{:S(2)}) collective-permute-start(f32[32,4224]{1,0:T(8,128)} %collective-permute-done.15.refs_2_.refs_12_), channel_id=1, source_target_pairs={{0,16},{16,0},{1,17},{17,1},{2,18},{18,2},{3,19},{19,3},{4,20},{20... | collective-permute-start | bytes 1622024 | tf_op jit(solution)/shard_map/ppermute | solution.py:76
  182.1 7.4 %collective-permute-start.30 = (f32[32,4224]{1,0:T(8,128)}, f32[32,4224]{1,0:T(8,128)}, u32[]{:S(2)}, u32[]{:S(2)}) collective-permute-start(f32[32,4224]{1,0:T(8,128)} %collective-permute-done.29.refs_8_), channel_id=1, source_target_pairs={{0,16},{16,0},{1,17},{17,1},{2,18},{18,2},{3,19},{19,3},{4,20},{20... | collective-permute-start | bytes 1622024 | tf_op jit(solution)/shard_map/ppermute | solution.py:76
  182.2 7.2 %collective-permute-start.28 = (f32[32,4224]{1,0:T(8,128)}, f32[32,4224]{1,0:T(8,128)}, u32[]{:S(2)}, u32[]{:S(2)}) collective-permute-start(f32[32,4224]{1,0:T(8,128)} %collective-permute-done.27.refs_7_), channel_id=1, source_target_pairs={{0,16},{16,0},{1,17},{17,1},{2,18},{18,2},{3,19},{19,3},{4,20},{20... | collective-permute-start | bytes 1622024 | tf_op jit(solution)/shard_map/ppermute | solution.py:76
  183.6 5.8 %collective-permute-start.32 = (f32[16,4224]{1,0:T(8,128)}, f32[16,4224]{1,0:T(8,128)}, u32[]{:S(2)}, u32[]{:S(2)}) collective-permute-start(f32[16,4224]{1,0:T(8,128)} %collective-permute-done.31.refs_9_), channel_id=1, source_target_pairs={{0,16},{16,0},{1,17},{17,1},{2,18},{18,2},{3,19},{19,3},{4,20},{20... | collective-permute-start | bytes 811016 | tf_op jit(solution)/shard_map/ppermute | solution.py:76
  (20 other events, 56.0 us)

commit v2 on v1

--- a/solution.py
+++ b/solution.py
@@ -204,7 +204,7 @@
     )(image, kernel, bias, gain, shift)
 
 
-def backward_kernel(gn, xhat, inv, gain, image, upstream, kernel, out, taps, pad, sums, acc):
+def backward_kernel(gn, xhat, inv, gain, image, pad, taps, sums, acc):
     pad[...] = jnp.zeros_like(pad)
     sums[...] = jnp.zeros_like(sums)
 
@@ -237,17 +237,17 @@
         lanes = pl.ds(pl.multiple_of(b * 128, 128), 128)
         acc[...] = jnp.zeros_like(acc)
 
-        @pl.loop(0, 16)
-        def _(h):
-            x = image[h, :, lanes].astype(jnp.float32)
-            back = upstream[h, :, lanes].astype(jnp.float32)
-            for i in range(7):
+        @pl.loop(0, 8)
+        def _(pair):
+            h = pair * 2
+            x = [image[h + k, :, lanes].astype(jnp.float32) for k in range(2)]
+            for r in range(8):
                 for j in range(7):
-                    t = i * 7 + j
-                    g = pad[b, h + 6 - i, pl.ds(11 - j, 48), :]
-                    back = back + g * kernel[i, j : j + 1, lanes]
-                    acc[t] += fold(g * x)
-            out[h, :, lanes] = back.astype(jnp.bfloat16)
+                    g = pad[b, h + r, pl.ds(11 - j, 48), :]
+                    for k in range(2):
+                        i = 6 + k - r
+                        if 0 <= i < 7:
+                            acc[i * 7 + j] += fold(g * x[k])
 
         for t in range(49):
             taps[t : t + 1, lanes] = jnp.sum(acc[t], axis=0, keepdims=True) * (1.0 / 256)
@@ -256,22 +256,51 @@
         taps[49 + t : 50 + t, :] = jnp.sum(sums[t], axis=0, keepdims=True) * (1.0 / 256)
 
 
-def backward(gn, xhat, inv, gain, image, upstream, kernel):
+def backward(gn, xhat, inv, gain, image):
     return pl.pallas_call(
         backward_kernel,
         out_shape=(
-            jax.ShapeDtypeStruct((16, 48, 512), jnp.bfloat16),
+            jax.ShapeDtypeStruct((4, 22, 64, 128), jnp.float32),
             jax.ShapeDtypeStruct((52, 512), jnp.float32),
         ),
         scratch_shapes=[
-            pltpu.VMEM((4, 22, 64, 128), jnp.float32),
             pltpu.VMEM((3, 8, 512), jnp.float32),
             pltpu.VMEM((49, 8, 128), jnp.float32),
         ],
         compiler_params=pltpu.CompilerParams(vmem_limit_bytes=40 << 20),
-        cost_estimate=pl.CostEstimate(flops=80000000, bytes_accessed=6000000, transcendentals=0),
+        cost_estimate=pl.CostEstimate(flops=40000000, bytes_accessed=6000000, transcendentals=0),
+        name="norm_back",
+    )(gn, xhat, inv, gain, image)
+
+
+def spread_kernel(pad, upstream, kernel, out):
+    @pl.loop(0, 4)
+    def _(b):
+        lanes = pl.ds(pl.multiple_of(b * 128, 128), 128)
+
+        @pl.loop(0, 4)
+        def _(group):
+            h = group * 4
+            back = [upstream[h + k, :, lanes].astype(jnp.float32) for k in range(4)]
+            for r in range(10):
+                for j in range(7):
+                    g = pad[b, h + r, pl.ds(11 - j, 48), :]
+                    for k in range(4):
+                        i = 6 + k - r
+                        if 0 <= i < 7:
+                            back[k] = back[k] + g * kernel[i, j : j + 1, lanes]
+            for k in range(4):
+                out[h + k, :, lanes] = back[k].astype(jnp.bfloat16)
+
+
+def spread(pad, upstream, kernel):
+    return pl.pallas_call(
+        spread_kernel,
+        out_shape=jax.ShapeDtypeStruct((16, 48, 512), jnp.bfloat16),
+        compiler_params=pltpu.CompilerParams(vmem_limit_bytes=16 << 20),
+        cost_estimate=pl.CostEstimate(flops=40000000, bytes_accessed=6000000, transcendentals=0),
         name="conv_back",
-    )(gn, xhat, inv, gain, image, upstream, kernel)
+    )(pad, upstream, kernel)
 
 
 def body(
@@ -302,14 +331,16 @@
     gb_send, gb_keep = own_half_last(g_branch)
     down_send = contract(gb_send, hidden) * scale
     down_keep = contract(gb_keep, hidden) * scale
-    down_mine = down_keep + lax.ppermute(down_send, "c", FLIP)
+    down_recv = lax.ppermute(down_send, "c", FLIP)
+    down_keep, down_recv = lax.optimization_barrier((down_keep, down_recv))
+    down_mine = down_keep + down_recv
 
     g_branch_b, pre, _ = lax.optimization_barrier((g_branch, pre, down_send))
+
+    down_mine, g_branch_b, pre = lax.optimization_barrier((down_mine, g_branch_b, pre))
+    moved = lax.all_to_all(down_mine.reshape(16, 16, 2048), PLANE, 0, 0, tiled=True)
     g_hidden = jnp.dot(g_branch_b, w_down, preferred_element_type=jnp.float32)
     g_pre = (g_hidden * gelu_slope(pre)).astype(jnp.bfloat16)
-
-    g_pre, down_mine = lax.optimization_barrier((g_pre, down_mine))
-    moved = lax.all_to_all(down_mine.reshape(16, 16, 2048), PLANE, 0, 0, tiled=True)
     norm_send, norm_keep = own_half_last(normalized_output)
     up_send = contract(norm_send, g_pre) * scale
     up_keep = contract(norm_keep, g_pre) * scale
@@ -319,16 +350,9 @@
     normalized_gradient = lax.dot_general(
         g_pre_b, w_up, (((1,), (1,)), ((), ())), preferred_element_type=jnp.float32
     )
-    grad_inputs, block = backward(
-        normalized_gradient,
-        standardized_input,
-        inverse_deviation,
-        gain_row,
-        image,
-        grad_out[0],
-        conv_kernel,
-    )
-    grad_inputs = grad_inputs.reshape(1, row_count, column_count, channel_count)
+    g_mixed, block = backward(
+        normalized_gradient, standardized_input, inverse_deviation, gain_row, image
+    )
 
     hidden_b, g_pre_c, grad_out_b, g_branch_c, _ = lax.optimization_barrier(
         (hidden, g_pre, grad_out, g_branch, up_keep)
@@ -349,12 +373,16 @@
     small_keep = jnp.where(c == 0, block[:32], block[32:])
     small_mine = small_keep + lax.ppermute(small_send, "c", FLIP)
     small_mine = small_mine.reshape(4, 8, 4, 128).transpose(2, 0, 1, 3).reshape(16, 8, 128)
-    small_mine = jnp.pad(small_mine, ((0, 0), (0, 8), (0, 0)))
-    up_mine = jnp.concatenate([(up_keep + up_recv).reshape(16, 16, 2048), small_mine], axis=2)
-
-    up_mine, moved, grad_inputs = lax.optimization_barrier((up_mine, moved, grad_inputs))
+    up_keep, up_recv, small_mine = lax.optimization_barrier((up_keep, up_recv, small_mine))
+    up_mine = jnp.pad((up_keep + up_recv).reshape(16, 16, 2048), ((0, 0), (0, 0), (0, 128)))
+    up_mine = lax.dynamic_update_slice(up_mine, small_mine, (0, 0, 2048))
+
+    up_mine, moved, g_mixed = lax.optimization_barrier((up_mine, moved, g_mixed))
     down_piece = jnp.sum(moved, axis=0)
-    up_piece = jnp.sum(lax.all_to_all(up_mine, PLANE, 0, 0, tiled=True), axis=0)
+    up_moved = lax.all_to_all(up_mine, PLANE, 0, 0, tiled=True)
+    up_piece = jnp.sum(up_moved, axis=0)
+    grad_inputs = spread(g_mixed, grad_out[0], conv_kernel)
+    grad_inputs = grad_inputs.reshape(1, row_count, column_count, channel_count)
     down_full = sum_z(down_piece)
 
     up_piece, down_full = lax.optimization_barrier((up_piece, down_full))

time: 196 us -> 203 us (1.036)
  starting transfers between devices: 60.9 us -> 72.2 us
  waiting for transfers between devices: 55.4 us -> 49.4 us
  local copies, waits for them, and re-layouts: 8.32 us -> 11.4 us
    all_to_all x1, waiting for transfers between devices: 0.01 us -> 7.58 us  [body(): lax.all_to_all(down_mine.reshape(16, 16, 2048), PLANE, 0, 0, tiled=True)]
    ppermute x6, waiting for transfers between devices: 7.49 us -> 1.02 us  [gather_near(): lax.ppermute(p, ax, RING4[s])]
    ppermute x10, starting transfers between devices: 14.5 us -> 20.6 us  [gather_rest(): return (out, [lax.ppermute(p, 'c', FLIP) for p in out])]
    all_to_all x1, waiting for transfers between devices: 9.74 us -> 4.41 us  [body(): up_moved = lax.all_to_all(up_mine, PLANE, 0, 0, tiled=True)]
    ppermute x6, starting transfers between devices: 3.29 us -> 6.77 us  [gather_near(): lax.ppermute(p, ax, RING4[s])]
    ppermute x2, waiting for transfers between devices: 4.3 us -> 1.59 us  [gather_sides(): lax.ppermute(p, ax, RING4[3])]
    ppermute x1, waiting for transfers between devices: 0.01 us -> 2.66 us  [body(): down_recv = lax.ppermute(down_send, 'c', FLIP)]
    ppermute x2, starting transfers between devices: 0.55 us -> 3.07 us  [gather_sides(): lax.ppermute(p, ax, RING4[3])]
  transfers between devices with their start and end apart: 37 -> 37, of which waited for: 16 -> 15; matrix products, arithmetic and copies ran while one was open for 12% -> 10% of each run, Pallas kernels for 10% -> 9%
where the time goes in v2:
time: 203 us
  starting transfers between devices  72.2 us (36%)
  waiting for transfers between devices  49.4 us (24%)
  Pallas kernels  34.1 us (17%)
  matrix products  22.4 us (11%)
  other arithmetic  11.9 us (6%)
  local copies, waits for them, and re-layouts  11.4 us (6%)
    ppermute x8, waiting for transfers between devices, from_z(): return lax.ppermute(v, 'z', [(i, i ^ k) for i in range(8)])  29 us
    ppermute x10, starting transfers between devices, gather_rest(): return (out, [lax.ppermute(p, 'c', FLIP) for p in out])  20.6 us
    ppermute x8, starting transfers between devices, from_z(): return lax.ppermute(v, 'z', [(i, i ^ k) for i in range(8)])  19.6 us
    pallas_call x2, Pallas kernels, call(): pl.pallas_call(lambda *refs: kernel(far, *refs), out_shape=tuple((jax.Sha...  10.9 us
    pallas_call x1, Pallas kernels, forward(): pl.pallas_call(forward_kernel, out_shape=(jax.ShapeDtypeStruct((768, 512)...  8.94 us
    pallas_call x1, Pallas kernels, backward(): pl.pallas_call(backward_kernel, out_shape=(jax.ShapeDtypeStruct((4, 22, 6...  7.78 us
    all_to_all x1, waiting for transfers between devices, body(): lax.all_to_all(down_mine.reshape(16, 16, 2048), PLANE, 0, 0, tiled=True)  7.58 us
    unnamed x70, local copies, waits for them, and re-layouts  7.16 us
  transfers between devices with their start and end apart: 37, of which 15 were waited for; matrix products, arithmetic and copies ran while one was open for 10% of the time, Pallas kernels for 9%

profile of v2, /device:TPU:1, one launch (start us, length us, event | category | flops | bytes accessed | tf_op | source)
XLA Modules:
  0.0 202.8 jit_solution(18278082200139924523)
XLA Ops:
  0.7 1.4 fusion.7
  2.1 1.4 copy-done.3
  6.5 8.9 %conv_norm.1 = (f32[768,512]{1,0:T(8,128)S(1)}, bf16[768,512]{1,0:T(8,128)(2,1)S(1)}, f32[768,1]{1,0:T(8,128)S(1)}) custom-call(bf16[16,48,512]{2,1,0:T(8,128)(2,1)S(1)} %bitcast.41, f32[7,7,512]{2,1,0:T(8,128)S(1)} %copy-done.9, f32[1,512]{1,0:T(1,128)S(1)} %bitcast.45, f32[1,512]{1,0:T(1,128)S(1)} %bitcast.43, f32[1,512]{1,0:T(1,128)S(1)} %bitcast.46), custom_call_target="tpu_custom_call" | custom-call | tf_op jit(solution)/shard_map/conv_norm/pallas_call | solution.py:194
  15.4 4.3 %multiply_convert_fusion = (bf16[768,2048]{1,0:T(8,128)(2,1)S(1)}, f32[768,2048]{1,0:T(8,128)S(1)}) fusion(f32[2048]{0:T(1024)} %param.18, bf16[768,512]{1,0:T(8,128)(2,1)S(1)} %get-tuple-element.46, bf16[512,2048]{1,0:T(8,128)(2,1)S(1)} %copy-done), kind=kOutput, calls=%fused_computation.8 | convolution fusion | flops 1620049920 | bytes 12328960 | tf_op jit(solution)/shard_map/dot_general | solution.py:326
  20.8 3.3 %collective-permute-start = (f32[256,2048]{1,0:T(8,128)S(1)}, f32[256,2048]{1,0:T(8,128)S(1)}, u32[]{:S(2)}, u32[]{:S(2)}) collective-permute-start(f32[256,2048]{1,0:T(8,128)S(1)} %convolution_multiply_fusion.2), channel_id=1, source_target_pairs={{0,16},{16,0},{1,17},{17,1},{2,18},{18,2},{3,19},{19,3},{4,20},{20... | collective-permute-start | bytes 6291464 | tf_op jit(solution)/shard_map/ppermute | solution.py:334
  25.2 2.7 %collective-permute-done = f32[256,2048]{1,0:T(8,128)S(1)} collective-permute-done((f32[256,2048]{1,0:T(8,128)S(1)}, f32[256,2048]{1,0:T(8,128)S(1)}, u32[]{:S(2)}, u32[]{:S(2)}) %collective-permute-start) | collective-permute-done | bytes 2097184 | tf_op jit(solution)/shard_map/ppermute | solution.py:334
  27.8 1.6 add.66
  29.4 3.8 %fusion.5 = bf16[768,2048]{1,0:T(8,128)(2,1)S(1)} fusion(f32[768,2048]{1,0:T(8,128)S(1)} %get-tuple-element.52, bf16[768,512]{1,0:T(8,128)(2,1)S(1)} %fusion.7, bf16[512,2048]{1,0:T(8,128)(2,1)S(1)} %copy-done.31), kind=kOutput, calls=%fused_computation.6 | convolution fusion | flops 1626341376 | bytes 12320768 | tf_op jit(solution)/shard_map/dot_general | solution.py:342
  33.2 2.4 %convolution_multiply_fusion.1 = f32[256,2048]{1,0:T(8,128)} fusion(bf16[768,2048]{1,0:T(8,128)(2,1)S(1)} %fusion.5, pred[]{:T(512)S(6)} %eq.2, bf16[768,512]{1,0:T(8,128)(2,1)S(1)} %get-tuple-element.46), kind=kOutput, calls=%fused_computation.11 | convolution fusion | flops 806027264 | bytes 6029313 | tf_op jit(solution)/shard_map/dot_general | solution.py:43
  35.6 2.4 %convolution_multiply_fusion = f32[256,2048]{1,0:T(8,128)} fusion(bf16[768,2048]{1,0:T(8,128)(2,1)S(1)} %fusion.5, pred[]{:T(512)S(6)} %eq.2, bf16[768,512]{1,0:T(8,128)(2,1)S(1)} %get-tuple-element.46), kind=kOutput, calls=%fused_computation.10 | convolution fusion | flops 806027264 | bytes 6029313 | tf_op jit(solution)/shard_map/dot_general | solution.py:43
  38.0 5.2 %all-to-all-start = ((f32[16,16,2048]{2,1,0:T(8,128)}), f32[16,16,2048]{2,1,0:T(8,128)}, u32[]{:S(2)}, u32[]{:S(2)}) async-start(f32[16,16,2048]{2,1,0:T(8,128)} %bitcast.47), calls=%async_computation | async-start | bytes 4194304 | tf_op jit(solution)/shard_map/all_to_all | solution.py:341
  44.0 2.5 %convert_reduce_fusion = f32[2048]{0:T(1024)S(1)} fusion(bf16[768,2048]{1,0:T(8,128)(2,1)} %copy-done.18), kind=kLoop, calls=%fused_computation.7 | loop fusion | flops 3143680 | bytes 3153920 | tf_op jit(solution)/shard_map/reduce_sum | solution.py:360
  46.7 3.7 %fusion.6 = f32[512]{0:T(512)S(1)} fusion(bf16[768,512]{1,0:T(8,128)(2,1)S(1)} %bitcast.39, bf16[768,2048]{1,0:T(8,128)(2,1)} %copy-done.34, bf16[512,2048]{1,0:T(8,128)(2,1)S(1)} %copy-done.32, f32[512]{0:T(512)S(1)} %copy-done.33), kind=kOutput, calls=%fused_computation.15 | convolution fusion | flops 1612185088 | bytes 6033408 | tf_op jit(solution)/shard_map/dot_general | solution.py:362
  50.5 3.9 %fusion.26.gn = f32[768,512]{1,0:T(8,128)S(1)} fusion(bf16[768,2048]{1,0:T(8,128)(2,1)} %copy-done.18, bf16[512,2048]{1,0:T(8,128)(2,1)S(1)} %copy-done), kind=kOutput, calls=%fused_computation.51 | convolution fusion | flops 1610612736 | bytes 6815744 | tf_op jit(solution)/shard_map/dot_general | solution.py:350
  54.4 7.8 %norm_back.1 = (f32[4,22,64,128]{3,2,1,0:T(8,128)S(1)}, f32[52,512]{1,0:T(8,128)S(1)}) custom-call(f32[768,512]{1,0:T(8,128)S(1)} %fusion.26.gn, f32[768,512]{1,0:T(8,128)S(1)} %copy-done.8, f32[768,1]{1,0:T(8,128)S(1)} %get-tuple-element.55.inv, f32[1,512]{1,0:T(1,128)S(1)} %bitcast.44, bf16[16,48,512]{2,1,0:T(8,128)(2,1)S(1)} %bitcast.42), custom_call_target="tpu_custom_call" | custom-call | flops 40000000 | bytes 6000000 | tf_op jit(solution)/shard_map/norm_back/pallas_call | solution.py:260
  63.8 1.9 add.72
  65.7 1.5 pad.4
  67.9 7.6 %all-to-all-done = f32[16,16,2048]{2,1,0:T(8,128)} async-done(((f32[16,16,2048]{2,1,0:T(8,128)}), f32[16,16,2048]{2,1,0:T(8,128)}, u32[]{:S(2)}, u32[]{:S(2)}) %all-to-all-start) | async-done | bytes 2097184 | tf_op jit(solution)/shard_map/all_to_all | solution.py:341
  75.5 4.4 %all-to-all-start.1 = ((f32[16,16,2176]{2,1,0:T(8,128)}), f32[16,16,2176]{2,1,0:T(8,128)}, u32[]{:S(2)}, u32[]{:S(2)}) async-start(f32[16,16,2176]{2,1,0:T(8,128)} %constant_dynamic-update-slice_fusion), calls=%async_computation.1 | async-start | bytes 4456448 | tf_op jit(solution)/shard_map/all_to_all | solution.py:382
  79.9 1.7 reduce_sum.49
  81.6 1.7 collective-permute-start.3
  83.3 2.8 %collective-permute-done.3 = f32[16,2048]{1,0:T(8,128)S(1)} collective-permute-done((f32[16,2048]{1,0:T(8,128)S(1)}, f32[16,2048]{1,0:T(8,128)S(1)}, u32[]{:S(2)}, u32[]{:S(2)}) %collective-permute-start.3) | collective-permute-done | bytes 131104 | tf_op jit(solution)/shard_map/ppermute | solution.py:50
  86.1 5.9 %collective-permute-start.6 = (f32[16,2048]{1,0:T(8,128)S(1)}, f32[16,2048]{1,0:T(8,128)S(1)}, u32[]{:S(2)}, u32[]{:S(2)}) collective-permute-start(f32[16,2048]{1,0:T(8,128)S(1)} %add.74), channel_id=1, source_target_pairs={{0,12},{2,14},{4,8},{6,10},{8,4},{10,6},{12,0},{14,2},{1,13},{3,15... | collective-permute-start | bytes 393224 | tf_op jit(solution)/shard_map/ppermute | solution.py:50
  94.2 2.2 %collective-permute-done.6 = f32[16,2048]{1,0:T(8,128)S(1)} collective-permute-done((f32[16,2048]{1,0:T(8,128)S(1)}, f32[16,2048]{1,0:T(8,128)S(1)}, u32[]{:S(2)}, u32[]{:S(2)}) %collective-permute-start.6) | collective-permute-done | bytes 131104 | tf_op jit(solution)/shard_map/ppermute | solution.py:50
  97.8 8.9 %collective-permute-done.4 = f32[16,2048]{1,0:T(8,128)S(1)} collective-permute-done((f32[16,2048]{1,0:T(8,128)S(1)}, f32[16,2048]{1,0:T(8,128)S(1)}, u32[]{:S(2)}, u32[]{:S(2)}) %collective-permute-start.4) | collective-permute-done | bytes 131104 | tf_op jit(solution)/shard_map/ppermute | solution.py:50
  106.8 4.4 %all-to-all-done.1 = f32[16,16,2176]{2,1,0:T(8,128)} async-done(((f32[16,16,2176]{2,1,0:T(8,128)}), f32[16,16,2176]{2,1,0:T(8,128)}, u32[]{:S(2)}, u32[]{:S(2)}) %all-to-all-start.1) | async-done | bytes 2228256 | tf_op jit(solution)/shard_map/all_to_all | solution.py:382
  111.2 1.7 reduce_sum.48
  112.9 1.7 collective-permute-start.7
  114.6 2.4 %collective-permute-done.7 = f32[16,2176]{1,0:T(8,128)S(1)} collective-permute-done((f32[16,2176]{1,0:T(8,128)S(1)}, f32[16,2176]{1,0:T(8,128)S(1)}, u32[]{:S(2)}, u32[]{:S(2)}) %collective-permute-start.7) | collective-permute-done | bytes 139296 | tf_op jit(solution)/shard_map/ppermute | solution.py:50
  117.1 5.9 %collective-permute-start.10 = (f32[16,2176]{1,0:T(8,128)S(1)}, f32[16,2176]{1,0:T(8,128)S(1)}, u32[]{:S(2)}, u32[]{:S(2)}) collective-permute-start(f32[16,2176]{1,0:T(8,128)S(1)} %add.78), channel_id=1, source_target_pairs={{0,12},{2,14},{4,8},{6,10},{8,4},{10,6},{12,0},{14,2},{1,13},{3,15... | collective-permute-start | bytes 417800 | tf_op jit(solution)/shard_map/ppermute | solution.py:50
  125.2 2.1 %collective-permute-done.10 = f32[16,2176]{1,0:T(8,128)S(1)} collective-permute-done((f32[16,2176]{1,0:T(8,128)S(1)}, f32[16,2176]{1,0:T(8,128)S(1)}, u32[]{:S(2)}, u32[]{:S(2)}) %collective-permute-start.10) | collective-permute-done | bytes 139296 | tf_op jit(solution)/shard_map/ppermute | solution.py:50
  127.3 3.6 %collective-permute-done.9 = f32[16,2176]{1,0:T(8,128)S(1)} collective-permute-done((f32[16,2176]{1,0:T(8,128)S(1)}, f32[16,2176]{1,0:T(8,128)S(1)}, u32[]{:S(2)}, u32[]{:S(2)}) %collective-permute-start.9) | collective-permute-done | bytes 139296 | tf_op jit(solution)/shard_map/ppermute | solution.py:50
  130.9 5.6 %collective-permute-done.8 = f32[16,2176]{1,0:T(8,128)S(1)} collective-permute-done((f32[16,2176]{1,0:T(8,128)S(1)}, f32[16,2176]{1,0:T(8,128)S(1)}, u32[]{:S(2)}, u32[]{:S(2)}) %collective-permute-start.8) | collective-permute-done | bytes 139296 | tf_op jit(solution)/shard_map/ppermute | solution.py:50
  139.1 3.0 %collective-permute-start.24 = (f32[8,4224]{1,0:T(8,128)S(1)}, f32[8,4224]{1,0:T(8,128)S(1)}, u32[]{:S(2)}, u32[]{:S(2)}) collective-permute-start(f32[8,4224]{1,0:T(8,128)S(1)} %get-tuple-element.82), channel_id=1, source_target_pairs={{0,32},{1,33},{32,0},{33,1},{2,34},{3,35},{34,2},{35,3},{4,36},{5,... | collective-permute-start | bytes 405512 | tf_op jit(solution)/shard_map/ppermute | solution.py:59
  145.0 4.5 %collective-permute-start.15 = (f32[32,4224]{1,0:T(8,128)S(1)}, f32[32,4224]{1,0:T(8,128)S(1)}, u32[]{:S(2)}, u32[]{:S(2)}) collective-permute-start(f32[32,4224]{1,0:T(8,128)S(1)} %pad_maximum_fusion.refs_1_.refs_11_), channel_id=1, source_target_pairs={{0,1},{1,32},{32,33},{33,0},{2,3},{3,34},{34,35},{35,2},{4,5},{5,3... | collective-permute-start | bytes 1622024 | tf_op jit(solution)/shard_map/ppermute | solution.py:66
  149.6 2.5 %collective-permute-start.29 = (f32[32,4224]{1,0:T(8,128)S(1)}, f32[32,4224]{1,0:T(8,128)}, u32[]{:S(2)}, u32[]{:S(2)}) collective-permute-start(f32[32,4224]{1,0:T(8,128)S(1)} %pad_maximum_fusion.1.refs_6_), channel_id=1, source_target_pairs={{0,192},{64,0},{128,64},{192,128},{1,193},{65,1},{129,65},{193,129... | collective-permute-start | bytes 1622024 | tf_op jit(solution)/shard_map/ppermute | solution.py:66
  152.1 5.7 %collective-permute-start.14 = (f32[32,4224]{1,0:T(8,128)S(1)}, f32[32,4224]{1,0:T(8,128)S(1)}, u32[]{:S(2)}, u32[]{:S(2)}) collective-permute-start(f32[32,4224]{1,0:T(8,128)S(1)} %pad_maximum_fusion.refs_1_.refs_11_), channel_id=1, source_target_pairs={{0,16},{16,0},{1,17},{17,1},{2,18},{18,2},{3,19},{19,3},{4,20},{20... | collective-permute-start | bytes 1622024 | tf_op jit(solution)/shard_map/ppermute | solution.py:76
  157.8 1.6 collective-permute-done.17.refs_3_.refs_13_
  159.4 3.2 %collective-permute-start.26 = (f32[32,4224]{1,0:T(8,128)S(1)}, f32[32,4224]{1,0:T(8,128)S(1)}, u32[]{:S(2)}, u32[]{:S(2)}) collective-permute-start(f32[32,4224]{1,0:T(8,128)S(1)} %pad_maximum_fusion.1.refs_6_), channel_id=1, source_target_pairs={{0,16},{16,0},{1,17},{17,1},{2,18},{18,2},{3,19},{19,3},{4,20},{20... | collective-permute-start | bytes 1622024 | tf_op jit(solution)/shard_map/ppermute | solution.py:76
  165.6 1.8 collective-permute-start.33
  168.4 1.8 collective-permute-done.21.refs_5_.refs_15_
  170.3 2.8 %collective-permute-start.22 = (f32[16,4224]{1,0:T(8,128)S(1)}, f32[16,4224]{1,0:T(8,128)S(1)}, u32[]{:S(2)}, u32[]{:S(2)}) collective-permute-start(f32[16,4224]{1,0:T(8,128)S(1)} %collective-permute-done.21.refs_5_.refs_15_), channel_id=1, source_target_pairs={{0,16},{16,0},{1,17},{17,1},{2,18},{18,2},{3,19},{19,3},{4,20},{20... | collective-permute-start | bytes 811016 | tf_op jit(solution)/shard_map/ppermute | solution.py:76
  173.9 2.0 collective-permute-start.34
  175.9 4.9 %collective-permute-start.16 = (f32[32,4224]{1,0:T(8,128)S(1)}, f32[32,4224]{1,0:T(8,128)}, u32[]{:S(2)}, u32[]{:S(2)}) collective-permute-start(f32[32,4224]{1,0:T(8,128)S(1)} %collective-permute-done.15.refs_2_.refs_12_), channel_id=1, source_target_pairs={{0,16},{16,0},{1,17},{17,1},{2,18},{18,2},{3,19},{19,3},{4,20},{20... | collective-permute-start | bytes 1622024 | tf_op jit(solution)/shard_map/ppermute | solution.py:76
  183.3 1.8 copy-done.6
  185.2 6.4 %conv_back.1 = bf16[16,48,512]{2,1,0:T(8,128)(2,1)} custom-call(f32[4,22,64,128]{3,2,1,0:T(8,128)S(1)} %copy-done.6, bf16[16,48,512]{2,1,0:T(8,128)(2,1)S(1)} %bitcast.40, f32[7,7,512]{2,1,0:T(8,128)S(1)} %copy-done.10), custom_call_target="tpu_custom_call" | custom-call | flops 40000000 | bytes 6000000 | tf_op jit(solution)/shard_map/conv_back/pallas_call | solution.py:297
  191.6 4.7 %shard_map.186 = (f32[512,2048]{1,0:T(8,128)}, f32[512,2048]{1,0:T(8,128)}) custom-call(s32[3]{0:T(128)} %pad_add_fusion.refs_0_, f32[32,4224]{1,0:T(8,128)} %copy-done.15, f32[32,4224]{1,0:T(8,128)} %copy-done.17, f32[32,4224]{1,0:T(8,128)} %copy-done.16, f32[16,4224]{1,0:T(8,128)} %copy-done.24, f32[16,4224]{1,0:T(8,128)} %copy-done.23, ...), custom_call_target="tpu_custom_call" | custom-call | tf_op jit(solution)/shard_map/pallas_call | solution.py:140
  196.4 6.2 %shard_map.187 = (f32[512,2048]{1,0:T(8,128)}, f32[512,2048]{1,0:T(8,128)}, f32[7,7,512]{2,1,0:T(8,128)}, f32[1,512]{1,0:T(1,128)}, f32[1,512]{1,0:T(1,128)}, /*...) custom-call(s32[3]{0:T(128)} %pad_add_fusion.refs_0_, ...), custom_call_target="tpu_custom_call", output_to_operand_aliasing={{0}: (16, {}), {1}: (17, {})} | custom-call | tf_op jit(solution)/shard_map/pallas_call | solution.py:140
  (137 shorter events, 27.0 us)
Async XLA Ops:
  0.6 14.8 %copy-start = (bf16[512,2048]{1,0:T(8,128)(2,1)S(1)}, bf16[512,2048]{1,0:T(8,128)(2,1)}, u32[]{:S(2)}) copy-start(bf16[512,2048]{1,0:T(8,128)(2,1)} %param.17) | copy-start | bytes 6291460
  2.1 27.3 %copy-start.19 = (bf16[768,512]{1,0:T(8,128)(2,1)}, bf16[768,512]{1,0:T(8,128)(2,1)S(1)}, u32[]{:S(2)}) copy-start(bf16[768,512]{1,0:T(8,128)(2,1)S(1)} %fusion.7) | copy-start | bytes 2359300
  20.8 7.1 %collective-permute-start = (f32[256,2048]{1,0:T(8,128)S(1)}, f32[256,2048]{1,0:T(8,128)S(1)}, u32[]{:S(2)}, u32[]{:S(2)}) collective-permute-start(f32[256,2048]{1,0:T(8,128)S(1)} %convolution_multiply_fusion.2), channel_id=1, source_target_pairs={{0,16},{16,0},{1,17},{17,1},{2,18},{18,2},{3,19},{19,3},{4,20},{20... | collective-permute-start | bytes 6291464 | tf_op jit(solution)/shard_map/ppermute | solution.py:334
  38.0 8.7 %copy-start.33 = (f32[512]{0:T(512)S(1)}, f32[512]{0:T(512)}, u32[]{:S(2)}) copy-start(f32[512]{0:T(512)} %param.20) | copy-start | bytes 6148
  38.0 37.4 %all-to-all-start = ((f32[16,16,2048]{2,1,0:T(8,128)}), f32[16,16,2048]{2,1,0:T(8,128)}, u32[]{:S(2)}, u32[]{:S(2)}) async-start(f32[16,16,2048]{2,1,0:T(8,128)} %bitcast.47), calls=%async_computation | async-start | bytes 4194304 | tf_op jit(solution)/shard_map/all_to_all | solution.py:341
  43.3 20.6 %collective-permute-start.1 = (f32[256,2048]{1,0:T(8,128)}, f32[256,2048]{1,0:T(8,128)}, u32[]{:S(2)}, u32[]{:S(2)}) collective-permute-start(f32[256,2048]{1,0:T(8,128)} %convolution_multiply_fusion), channel_id=1, source_target_pairs={{0,16},{16,0},{1,17},{17,1},{2,18},{18,2},{3,19},{19,3},{4,20},{20... | collective-permute-start | bytes 6291464 | tf_op jit(solution)/shard_map/ppermute | solution.py:347
  54.3 9.5 %copy-start.22 = (f32[256,2048]{1,0:T(8,128)S(1)}, f32[256,2048]{1,0:T(8,128)}, u32[]{:S(2)}) copy-start(f32[256,2048]{1,0:T(8,128)} %convolution_multiply_fusion.1) | copy-start | bytes 6291460
  62.3 1.5 collective-permute-start.2
  75.5 35.7 %all-to-all-start.1 = ((f32[16,16,2176]{2,1,0:T(8,128)}), f32[16,16,2176]{2,1,0:T(8,128)}, u32[]{:S(2)}, u32[]{:S(2)}) async-start(f32[16,16,2176]{2,1,0:T(8,128)} %constant_dynamic-update-slice_fusion), calls=%async_computation.1 | async-start | bytes 4456448 | tf_op jit(solution)/shard_map/all_to_all | solution.py:382
  81.6 4.5 %collective-permute-start.3 = (f32[16,2048]{1,0:T(8,128)S(1)}, f32[16,2048]{1,0:T(8,128)S(1)}, u32[]{:S(2)}, u32[]{:S(2)}) collective-permute-start(f32[16,2048]{1,0:T(8,128)S(1)} %reduce_sum.49), channel_id=1, source_target_pairs={{0,2},{2,0},{4,6},{6,4},{8,10},{10,8},{12,14},{14,12},{1,3},{3,1},... | collective-permute-start | bytes 393224 | tf_op jit(solution)/shard_map/ppermute | solution.py:50
  86.1 10.3 %collective-permute-start.6 = (f32[16,2048]{1,0:T(8,128)S(1)}, f32[16,2048]{1,0:T(8,128)S(1)}, u32[]{:S(2)}, u32[]{:S(2)}) collective-permute-start(f32[16,2048]{1,0:T(8,128)S(1)} %add.74), channel_id=1, source_target_pairs={{0,12},{2,14},{4,8},{6,10},{8,4},{10,6},{12,0},{14,2},{1,13},{3,15... | collective-permute-start | bytes 393224 | tf_op jit(solution)/shard_map/ppermute | solution.py:50
  92.0 5.8 %collective-permute-start.5 = (f32[16,2048]{1,0:T(8,128)S(1)}, f32[16,2048]{1,0:T(8,128)S(1)}, u32[]{:S(2)}, u32[]{:S(2)}) collective-permute-start(f32[16,2048]{1,0:T(8,128)S(1)} %add.74), channel_id=1, source_target_pairs={{0,4},{2,6},{4,0},{6,2},{8,12},{10,14},{12,8},{14,10},{1,5},{3,7},... | collective-permute-start | bytes 393224 | tf_op jit(solution)/shard_map/ppermute | solution.py:50
  93.2 13.5 %collective-permute-start.4 = (f32[16,2048]{1,0:T(8,128)S(1)}, f32[16,2048]{1,0:T(8,128)S(1)}, u32[]{:S(2)}, u32[]{:S(2)}) collective-permute-start(f32[16,2048]{1,0:T(8,128)S(1)} %add.74), channel_id=1, source_target_pairs={{0,8},{2,10},{4,12},{6,14},{8,0},{10,2},{12,4},{14,6},{1,9},{3,11}... | collective-permute-start | bytes 393224 | tf_op jit(solution)/shard_map/ppermute | solution.py:50
  112.9 70.4 %copy-start.10 = (f32[7,7,512]{2,1,0:T(8,128)S(1)}, f32[7,7,512]{2,1,0:T(8,128)}, u32[]{:S(2)}) copy-start(f32[7,7,512]{2,1,0:T(8,128)} %kernel.3) | copy-start | bytes 301060
  112.9 4.1 %collective-permute-start.7 = (f32[16,2176]{1,0:T(8,128)S(1)}, f32[16,2176]{1,0:T(8,128)S(1)}, u32[]{:S(2)}, u32[]{:S(2)}) collective-permute-start(f32[16,2176]{1,0:T(8,128)S(1)} %reduce_sum.48), channel_id=1, source_target_pairs={{0,2},{2,0},{4,6},{6,4},{8,10},{10,8},{12,14},{14,12},{1,3},{3,1},... | collective-permute-start | bytes 417800 | tf_op jit(solution)/shard_map/ppermute | solution.py:50
  117.1 10.2 %collective-permute-start.10 = (f32[16,2176]{1,0:T(8,128)S(1)}, f32[16,2176]{1,0:T(8,128)S(1)}, u32[]{:S(2)}, u32[]{:S(2)}) collective-permute-start(f32[16,2176]{1,0:T(8,128)S(1)} %add.78), channel_id=1, source_target_pairs={{0,12},{2,14},{4,8},{6,10},{8,4},{10,6},{12,0},{14,2},{1,13},{3,15... | collective-permute-start | bytes 417800 | tf_op jit(solution)/shard_map/ppermute | solution.py:50
  123.0 7.9 %collective-permute-start.9 = (f32[16,2176]{1,0:T(8,128)S(1)}, f32[16,2176]{1,0:T(8,128)S(1)}, u32[]{:S(2)}, u32[]{:S(2)}) collective-permute-start(f32[16,2176]{1,0:T(8,128)S(1)} %add.78), channel_id=1, source_target_pairs={{0,4},{2,6},{4,0},{6,2},{8,12},{10,14},{12,8},{14,10},{1,5},{3,7},... | collective-permute-start | bytes 417800 | tf_op jit(solution)/shard_map/ppermute | solution.py:50
  124.2 12.3 %collective-permute-start.8 = (f32[16,2176]{1,0:T(8,128)S(1)}, f32[16,2176]{1,0:T(8,128)S(1)}, u32[]{:S(2)}, u32[]{:S(2)}) collective-permute-start(f32[16,2176]{1,0:T(8,128)S(1)} %add.78), channel_id=1, source_target_pairs={{0,8},{2,10},{4,12},{6,14},{8,0},{10,2},{12,4},{14,6},{1,9},{3,11}... | collective-permute-start | bytes 417800 | tf_op jit(solution)/shard_map/ppermute | solution.py:50
  136.6 5.6 %collective-permute-start.13 = (f32[8,4224]{1,0:T(8,128)S(1)}, f32[8,4224]{1,0:T(8,128)S(1)}, u32[]{:S(2)}, u32[]{:S(2)}) collective-permute-start(f32[8,4224]{1,0:T(8,128)S(1)} %get-tuple-element.83), channel_id=1, source_target_pairs={{0,192},{64,0},{128,64},{192,128},{1,193},{65,1},{129,65},{193,129... | collective-permute-start | bytes 405512 | tf_op jit(solution)/shard_map/ppermute | solution.py:59
  137.7 5.6 %collective-permute-start.12 = (f32[8,4224]{1,0:T(8,128)S(1)}, f32[8,4224]{1,0:T(8,128)S(1)}, u32[]{:S(2)}, u32[]{:S(2)}) collective-permute-start(f32[8,4224]{1,0:T(8,128)S(1)} %get-tuple-element.83), channel_id=1, source_target_pairs={{0,128},{64,192},{128,0},{192,64},{1,129},{65,193},{129,1},{193,65... | collective-permute-start | bytes 405512 | tf_op jit(solution)/shard_map/ppermute | solution.py:59
  137.7 6.6 %collective-permute-start.11 = (f32[8,4224]{1,0:T(8,128)S(1)}, f32[8,4224]{1,0:T(8,128)S(1)}, u32[]{:S(2)}, u32[]{:S(2)}) collective-permute-start(f32[8,4224]{1,0:T(8,128)S(1)} %get-tuple-element.83), channel_id=1, source_target_pairs={{0,64},{64,128},{128,192},{192,0},{1,65},{65,129},{129,193},{193,1... | collective-permute-start | bytes 405512 | tf_op jit(solution)/shard_map/ppermute | solution.py:59
  138.4 11.1 %collective-permute-start.25 = (f32[8,4224]{1,0:T(8,128)S(1)}, f32[8,4224]{1,0:T(8,128)S(1)}, u32[]{:S(2)}, u32[]{:S(2)}) collective-permute-start(f32[8,4224]{1,0:T(8,128)S(1)} %get-tuple-element.82), channel_id=1, source_target_pairs={{0,33},{1,0},{32,1},{33,32},{2,35},{3,2},{34,3},{35,34},{4,37},{5,... | collective-permute-start | bytes 405512 | tf_op jit(solution)/shard_map/ppermute | solution.py:59
  139.1 10.4 %collective-permute-start.24 = (f32[8,4224]{1,0:T(8,128)S(1)}, f32[8,4224]{1,0:T(8,128)S(1)}, u32[]{:S(2)}, u32[]{:S(2)}) collective-permute-start(f32[8,4224]{1,0:T(8,128)S(1)} %get-tuple-element.82), channel_id=1, source_target_pairs={{0,32},{1,33},{32,0},{33,1},{2,34},{3,35},{34,2},{35,3},{4,36},{5,... | collective-permute-start | bytes 405512 | tf_op jit(solution)/shard_map/ppermute | solution.py:59
  142.2 7.3 %collective-permute-start.23 = (f32[8,4224]{1,0:T(8,128)S(1)}, f32[8,4224]{1,0:T(8,128)S(1)}, u32[]{:S(2)}, u32[]{:S(2)}) collective-permute-start(f32[8,4224]{1,0:T(8,128)S(1)} %get-tuple-element.82), channel_id=1, source_target_pairs={{0,1},{1,32},{32,33},{33,0},{2,3},{3,34},{34,35},{35,2},{4,5},{5,3... | collective-permute-start | bytes 405512 | tf_op jit(solution)/shard_map/ppermute | solution.py:59
  144.4 47.2 %copy-start.15 = (f32[32,4224]{1,0:T(8,128)}, f32[32,4224]{1,0:T(8,128)S(1)}, u32[]{:S(2)}) copy-start(f32[32,4224]{1,0:T(8,128)S(1)} %pad_maximum_fusion.refs_1_.refs_11_) | copy-start | bytes 1622020
  144.4 15.0 %collective-permute-start.17 = (f32[32,4224]{1,0:T(8,128)S(1)}, f32[32,4224]{1,0:T(8,128)S(1)}, u32[]{:S(2)}, u32[]{:S(2)}) collective-permute-start(f32[32,4224]{1,0:T(8,128)S(1)} %pad_maximum_fusion.refs_1_.refs_11_), channel_id=1, source_target_pairs={{0,33},{1,0},{32,1},{33,32},{2,35},{3,2},{34,3},{35,34},{4,37},{5,... | collective-permute-start | bytes 1622024 | tf_op jit(solution)/shard_map/ppermute | solution.py:66
  145.0 17.7 %collective-permute-start.15 = (f32[32,4224]{1,0:T(8,128)S(1)}, f32[32,4224]{1,0:T(8,128)S(1)}, u32[]{:S(2)}, u32[]{:S(2)}) collective-permute-start(f32[32,4224]{1,0:T(8,128)S(1)} %pad_maximum_fusion.refs_1_.refs_11_), channel_id=1, source_target_pairs={{0,1},{1,32},{32,33},{33,0},{2,3},{3,34},{34,35},{35,2},{4,5},{5,3... | collective-permute-start | bytes 1622024 | tf_op jit(solution)/shard_map/ppermute | solution.py:66
  149.6 42.0 %copy-start.21 = (f32[32,4224]{1,0:T(8,128)}, f32[32,4224]{1,0:T(8,128)S(1)}, u32[]{:S(2)}) copy-start(f32[32,4224]{1,0:T(8,128)S(1)} %pad_maximum_fusion.1.refs_6_) | copy-start | bytes 1622020
  149.6 14.0 %collective-permute-start.29 = (f32[32,4224]{1,0:T(8,128)S(1)}, f32[32,4224]{1,0:T(8,128)}, u32[]{:S(2)}, u32[]{:S(2)}) collective-permute-start(f32[32,4224]{1,0:T(8,128)S(1)} %pad_maximum_fusion.1.refs_6_), channel_id=1, source_target_pairs={{0,192},{64,0},{128,64},{192,128},{1,193},{65,1},{129,65},{193,129... | collective-permute-start | bytes 1622024 | tf_op jit(solution)/shard_map/ppermute | solution.py:66
  152.1 13.5 %collective-permute-start.27 = (f32[32,4224]{1,0:T(8,128)S(1)}, f32[32,4224]{1,0:T(8,128)}, u32[]{:S(2)}, u32[]{:S(2)}) collective-permute-start(f32[32,4224]{1,0:T(8,128)S(1)} %pad_maximum_fusion.1.refs_6_), channel_id=1, source_target_pairs={{0,64},{64,128},{128,192},{192,0},{1,65},{65,129},{129,193},{193,1... | collective-permute-start | bytes 1622024 | tf_op jit(solution)/shard_map/ppermute | solution.py:66
  152.1 16.2 %collective-permute-start.14 = (f32[32,4224]{1,0:T(8,128)S(1)}, f32[32,4224]{1,0:T(8,128)S(1)}, u32[]{:S(2)}, u32[]{:S(2)}) collective-permute-start(f32[32,4224]{1,0:T(8,128)S(1)} %pad_maximum_fusion.refs_1_.refs_11_), channel_id=1, source_target_pairs={{0,16},{16,0},{1,17},{17,1},{2,18},{18,2},{3,19},{19,3},{4,20},{20... | collective-permute-start | bytes 1622024 | tf_op jit(solution)/shard_map/ppermute | solution.py:76
  159.4 32.2 %copy-start.16 = (f32[32,4224]{1,0:T(8,128)}, f32[32,4224]{1,0:T(8,128)S(1)}, u32[]{:S(2)}) copy-start(f32[32,4224]{1,0:T(8,128)S(1)} %collective-permute-done.17.refs_3_.refs_13_) | copy-start | bytes 1622020
  159.4 14.4 %collective-permute-start.26 = (f32[32,4224]{1,0:T(8,128)S(1)}, f32[32,4224]{1,0:T(8,128)S(1)}, u32[]{:S(2)}, u32[]{:S(2)}) collective-permute-start(f32[32,4224]{1,0:T(8,128)S(1)} %pad_maximum_fusion.1.refs_6_), channel_id=1, source_target_pairs={{0,16},{16,0},{1,17},{17,1},{2,18},{18,2},{3,19},{19,3},{4,20},{20... | collective-permute-start | bytes 1622024 | tf_op jit(solution)/shard_map/ppermute | solution.py:76
  162.7 28.9 %copy-start.17 = (f32[32,4224]{1,0:T(8,128)}, f32[32,4224]{1,0:T(8,128)S(1)}, u32[]{:S(2)}) copy-start(f32[32,4224]{1,0:T(8,128)S(1)} %collective-permute-done.15.refs_2_.refs_12_) | copy-start | bytes 1622020
  162.7 7.6 %collective-permute-start.21 = (f32[16,4224]{1,0:T(8,128)S(1)}, f32[16,4224]{1,0:T(8,128)S(1)}, u32[]{:S(2)}, u32[]{:S(2)}) collective-permute-start(f32[16,4224]{1,0:T(8,128)S(1)} %slice.56), channel_id=1, source_target_pairs={{0,33},{1,0},{32,1},{33,32},{2,35},{3,2},{34,3},{35,34},{4,37},{5,... | collective-permute-start | bytes 811016 | tf_op jit(solution)/shard_map/ppermute | solution.py:74
  163.6 9.5 %collective-permute-start.19 = (f32[16,4224]{1,0:T(8,128)S(1)}, f32[16,4224]{1,0:T(8,128)S(1)}, u32[]{:S(2)}, u32[]{:S(2)}) collective-permute-start(f32[16,4224]{1,0:T(8,128)S(1)} %slice.55), channel_id=1, source_target_pairs={{0,1},{1,32},{32,33},{33,0},{2,3},{3,34},{34,35},{35,2},{4,5},{5,3... | collective-permute-start | bytes 811016 | tf_op jit(solution)/shard_map/ppermute | solution.py:74
  165.6 8.3 %collective-permute-start.33 = (f32[16,4224]{1,0:T(8,128)S(1)}, f32[16,4224]{1,0:T(8,128)S(1)}, u32[]{:S(2)}, u32[]{:S(2)}) collective-permute-start(f32[16,4224]{1,0:T(8,128)S(1)} %slice.58), channel_id=1, source_target_pairs={{0,192},{64,0},{128,64},{192,128},{1,193},{65,1},{129,65},{193,129... | collective-permute-start | bytes 811016 | tf_op jit(solution)/shard_map/ppermute | solution.py:74
  168.3 12.5 %copy-start.25 = (f32[32,4224]{1,0:T(8,128)}, f32[32,4224]{1,0:T(8,128)S(1)}, u32[]{:S(2)}) copy-start(f32[32,4224]{1,0:T(8,128)S(1)} %collective-permute-done.14.refs_1_) | copy-start | bytes 1622020
  168.3 7.6 %collective-permute-start.31 = (f32[16,4224]{1,0:T(8,128)S(1)}, f32[16,4224]{1,0:T(8,128)}, u32[]{:S(2)}, u32[]{:S(2)}) collective-permute-start(f32[16,4224]{1,0:T(8,128)S(1)} %slice.57), channel_id=1, source_target_pairs={{0,64},{64,128},{128,192},{192,0},{1,65},{65,129},{129,193},{193,1... | collective-permute-start | bytes 811016 | tf_op jit(solution)/shard_map/ppermute | solution.py:74
  170.3 21.3 %copy-start.23 = (f32[16,4224]{1,0:T(8,128)}, f32[16,4224]{1,0:T(8,128)S(1)}, u32[]{:S(2)}) copy-start(f32[16,4224]{1,0:T(8,128)S(1)} %collective-permute-done.21.refs_5_.refs_15_) | copy-start | bytes 811012
  170.3 10.5 %collective-permute-start.22 = (f32[16,4224]{1,0:T(8,128)S(1)}, f32[16,4224]{1,0:T(8,128)S(1)}, u32[]{:S(2)}, u32[]{:S(2)}) collective-permute-start(f32[16,4224]{1,0:T(8,128)S(1)} %collective-permute-done.21.refs_5_.refs_15_), channel_id=1, source_target_pairs={{0,16},{16,0},{1,17},{17,1},{2,18},{18,2},{3,19},{19,3},{4,20},{20... | collective-permute-start | bytes 811016 | tf_op jit(solution)/shard_map/ppermute | solution.py:76
  173.1 7.8 %collective-permute-start.20 = (f32[16,4224]{1,0:T(8,128)S(1)}, f32[16,4224]{1,0:T(8,128)S(1)}, u32[]{:S(2)}, u32[]{:S(2)}) collective-permute-start(f32[16,4224]{1,0:T(8,128)S(1)} %collective-permute-done.19.refs_4_.refs_14_), channel_id=1, source_target_pairs={{0,16},{16,0},{1,17},{17,1},{2,18},{18,2},{3,19},{19,3},{4,20},{20... | collective-permute-start | bytes 811016 | tf_op jit(solution)/shard_map/ppermute | solution.py:76
  173.8 22.6 %collective-permute-start.18 = (f32[32,4224]{1,0:T(8,128)S(1)}, f32[32,4224]{1,0:T(8,128)}, u32[]{:S(2)}, u32[]{:S(2)}) collective-permute-start(f32[32,4224]{1,0:T(8,128)S(1)} %collective-permute-done.17.refs_3_.refs_13_), channel_id=1, source_target_pairs={{0,16},{16,0},{1,17},{17,1},{2,18},{18,2},{3,19},{19,3},{4,20},{20... | collective-permute-start | bytes 1622024 | tf_op jit(solution)/shard_map/ppermute | solution.py:76
  173.9 7.6 %collective-permute-start.34 = (f32[16,4224]{1,0:T(8,128)S(1)}, f32[16,4224]{1,0:T(8,128)S(1)}, u32[]{:S(2)}, u32[]{:S(2)}) collective-permute-start(f32[16,4224]{1,0:T(8,128)S(1)} %collective-permute-done.33.refs_10_), channel_id=1, source_target_pairs={{0,16},{16,0},{1,17},{17,1},{2,18},{18,2},{3,19},{19,3},{4,20},{20... | collective-permute-start | bytes 811016 | tf_op jit(solution)/shard_map/ppermute | solution.py:76
  175.9 20.5 %collective-permute-start.16 = (f32[32,4224]{1,0:T(8,128)S(1)}, f32[32,4224]{1,0:T(8,128)}, u32[]{:S(2)}, u32[]{:S(2)}) collective-permute-start(f32[32,4224]{1,0:T(8,128)S(1)} %collective-permute-done.15.refs_2_.refs_12_), channel_id=1, source_target_pairs={{0,16},{16,0},{1,17},{17,1},{2,18},{18,2},{3,19},{19,3},{4,20},{20... | collective-permute-start | bytes 1622024 | tf_op jit(solution)/shard_map/ppermute | solution.py:76
  180.7 15.6 %collective-permute-start.30 = (f32[32,4224]{1,0:T(8,128)}, f32[32,4224]{1,0:T(8,128)}, u32[]{:S(2)}, u32[]{:S(2)}) collective-permute-start(f32[32,4224]{1,0:T(8,128)} %collective-permute-done.29.refs_8_), channel_id=1, source_target_pairs={{0,16},{16,0},{1,17},{17,1},{2,18},{18,2},{3,19},{19,3},{4,20},{20... | collective-permute-start | bytes 1622024 | tf_op jit(solution)/shard_map/ppermute | solution.py:76
  180.9 15.5 %collective-permute-start.28 = (f32[32,4224]{1,0:T(8,128)}, f32[32,4224]{1,0:T(8,128)}, u32[]{:S(2)}, u32[]{:S(2)}) collective-permute-start(f32[32,4224]{1,0:T(8,128)} %collective-permute-done.27.refs_7_), channel_id=1, source_target_pairs={{0,16},{16,0},{1,17},{17,1},{2,18},{18,2},{3,19},{19,3},{4,20},{20... | collective-permute-start | bytes 1622024 | tf_op jit(solution)/shard_map/ppermute | solution.py:76
  182.3 14.0 %collective-permute-start.32 = (f32[16,4224]{1,0:T(8,128)}, f32[16,4224]{1,0:T(8,128)}, u32[]{:S(2)}, u32[]{:S(2)}) collective-permute-start(f32[16,4224]{1,0:T(8,128)} %collective-permute-done.31.refs_9_), channel_id=1, source_target_pairs={{0,16},{16,0},{1,17},{17,1},{2,18},{18,2},{3,19},{19,3},{4,20},{20... | collective-permute-start | bytes 811016 | tf_op jit(solution)/shard_map/ppermute | solution.py:76
  (24 other events, 86.8 us)
